TPU v7x, 256 devices: a whole 4x4x8 slice. The times are simulated.
256 devices in a mesh: row: 16 (over x, y), col: 16 (over z, core).
Axes of the slice: x: 4, y: 4, z: 8, core: 2. Of those that a mesh axis runs over, the one named last changes fastest.
Arguments:
- tokens: bfloat16 [512, 8192], P('col', 'row'), may hold values from -6 to 6
- cotangent: bfloat16 [512, 8192], P('col', 'row'), may hold values from -6 to 6
- gate_weight: bfloat16 [8192, 32768], P('row', 'col'), may hold values from -0.125 to 0.125
- up_weight: bfloat16 [8192, 32768], P('row', 'col'), may hold values from -0.125 to 0.125
- down_weight: bfloat16 [32768, 8192], P('col', 'row'), may hold values from -0.0625 to 0.0625
- block_mask: int32 [3, 16, 64], P(None, 'row', 'col'), may hold values 0 or 1
Outputs:
- input_grad: bfloat16 [512, 8192], P('col', 'row')
- gate_grad: bfloat16 [8192, 32768], P('row', 'col')
- up_grad: bfloat16 [8192, 32768], P('row', 'col')
- down_grad: bfloat16 [32768, 8192], P('col', 'row')
All inputs are finite; a program needn't handle non-finite values. No bound on the sum of `block_mask` on one device may be relied on, other than what follows from the above.
Results may differ from a plain program's by a relative error of at most 0.005.
Values may be sent and summed in bfloat16 or wider, within the bound.
No kernel may reach another device: no remote copies, remote signals or barrier semaphores. Data moves between devices by JAX's collectives and lax.ppermute only.
A program may use at most 128 MiB of HBM per device.

v0:
```python
import jax
import jax.numpy as jnp
from jax import lax
from jax.experimental import pallas as pl
from jax.experimental.pallas import tpu as pltpu
from jax.sharding import Mesh, PartitionSpec as P


BLK = 512
VMEM_LIMIT = 20 * 2**20
F32 = jnp.float32
BF16 = jnp.bfloat16

PAIRS_LOW = [(0, 1), (1, 0), (2, 3), (3, 2)]
PAIRS_HIGH = [(1, 2), (2, 1), (3, 0), (0, 3)]
DIMS = (("x", PAIRS_LOW), ("x", PAIRS_HIGH), ("y", PAIRS_LOW), ("y", PAIRS_HIGH))
ORDERS = ((0, 1, 2, 3), (1, 0, 3, 2), (2, 3, 0, 1), (3, 2, 1, 0))
QUARTERS = len(ORDERS)
NODES = 16
GROUP = 8


def exchange(value, dim):
    axis, pairs = DIMS[dim]
    return lax.ppermute(value, axis, pairs)


def block_order(order):
    kept = [0]
    for dim in reversed(order):
        sent = [p ^ (1 << dim) for p in kept]
        kept = sent + kept
    return kept


def token_places():
    half = NODES // 2
    orders = [block_order(order) for order in ORDERS]
    places = [q * NODES + p for q in range(QUARTERS) for p in orders[q][:half]]
    places += [q * NODES + p for q in range(QUARTERS) for p in orders[q][half:]]
    return places


def dot(a, b, contract):
    return lax.dot_general(a, b, ((contract[:1], contract[1:]), ((), ())), preferred_element_type=F32)


def forward_kernel(mask, tok, cot, gate, up, down, *refs):
    outs = refs[:QUARTERS]
    buffers, sems = refs[QUARTERS:-1], refs[-1]
    f = pl.program_id(0)
    rows = outs[0].shape[1]

    def fetch(m, at):
        cut = pl.ds(at * BLK, BLK)
        source = (gate.at[:, cut], up.at[:, cut], down.at[cut, :])[m]
        return pltpu.make_async_copy(source, buffers[m].at[at], sems.at[m, at])

    @pl.when(f == 0)
    def _():
        for at in range(buffers[0].shape[0]):
            for m in range(3):
                fetch(m, at).start()

    for m, (value, contract) in enumerate(((tok, (1, 0)), (tok, (1, 0)), (cot, (1, 1)))):
        fetch(m, f).wait()

        @pl.when(mask[m, f] != 0)
        def _():
            product = dot(value[...], buffers[m][f], contract)
            for q, out in enumerate(outs):
                out[m] = product[q * rows : (q + 1) * rows].astype(out.dtype)

        @pl.when(mask[m, f] == 0)
        def _():
            for out in outs:
                out[m] = jnp.zeros(out.shape[1:], out.dtype)


def forward(mask, permuted, half, gate, up, down, dtype):
    count, both = permuted.shape
    rows, width = count // 2, both // 2
    hidden = gate.shape[1]
    blocks = hidden // BLK
    share = rows // QUARTERS
    return pl.pallas_call(
        forward_kernel,
        grid_spec=pltpu.PrefetchScalarGridSpec(
            num_scalar_prefetch=1,
            grid=(blocks,),
            in_specs=[
                pl.BlockSpec((rows, width), lambda f, mask: (half, 0)),
                pl.BlockSpec((rows, width), lambda f, mask: (half, 1)),
            ]
            + [pl.BlockSpec(memory_space=pl.ANY)] * 3,
            out_specs=[pl.BlockSpec((3, share, BLK), lambda f, mask: (0, 0, f))] * QUARTERS,
            scratch_shapes=[
                pltpu.VMEM((blocks, width, BLK), BF16),
                pltpu.VMEM((blocks, width, BLK), BF16),
                pltpu.VMEM((blocks, BLK, width), BF16),
                pltpu.SemaphoreType.DMA((3, blocks)),
            ],
        ),
        out_shape=[jax.ShapeDtypeStruct((3, share, hidden), dtype)] * QUARTERS,
        compiler_params=pltpu.CompilerParams(vmem_limit_bytes=VMEM_LIMIT),
        cost_estimate=pl.CostEstimate(
            flops=6 * rows * width * hidden,
            transcendentals=0,
            bytes_accessed=6 * width * hidden + 3 * rows * hidden * jnp.dtype(dtype).itemsize,
        ),
    )(mask, permuted, permuted, gate, up, down)


def whole(far, near, m_far, m_near):
    return jnp.concatenate([piece[m_far] for piece in far] + [piece[m_near] for piece in near], axis=0)


def input_kernel(mask, places, gate, up, *refs):
    far, near = refs[:QUARTERS], refs[QUARTERS : 2 * QUARTERS]
    input_grad, acc = refs[2 * QUARTERS :]
    f = pl.program_id(0)

    @pl.when(f == 0)
    def _():
        acc[...] = jnp.zeros_like(acc)

    for m, weight in enumerate((gate, up)):

        @pl.when(mask[m, f] != 0)
        def _():
            acc[...] += dot(whole(far, near, m, m), weight[...], (1, 1))

    @pl.when(f == pl.num_programs(0) - 1)
    def _():
        for i in range(input_grad.shape[0]):
            input_grad[places[i]] = acc[i * GROUP : (i + 1) * GROUP]


def input_gradient(mask, places, gate, up, far, near):
    width, hidden = gate.shape
    share = near[0].shape[1]
    rows = 2 * QUARTERS * share
    groups = rows // GROUP
    return pl.pallas_call(
        input_kernel,
        name="input_gradient",
        grid_spec=pltpu.PrefetchScalarGridSpec(
            num_scalar_prefetch=2,
            grid=(hidden // BLK,),
            in_specs=[pl.BlockSpec((width, BLK), lambda f, *_: (0, f))] * 2
            + [pl.BlockSpec((2, share, BLK), lambda f, *_: (0, 0, f))] * QUARTERS
            + [pl.BlockSpec((3, share, BLK), lambda f, *_: (0, 0, f))] * QUARTERS,
            out_specs=pl.BlockSpec((groups, GROUP, width), lambda f, *_: (0, 0, 0)),
            scratch_shapes=[pltpu.VMEM((rows, width), F32)],
        ),
        out_shape=jax.ShapeDtypeStruct((groups, GROUP, width), F32),
        compiler_params=pltpu.CompilerParams(vmem_limit_bytes=VMEM_LIMIT),
        cost_estimate=pl.CostEstimate(
            flops=4 * rows * width * hidden,
            transcendentals=0,
            bytes_accessed=4 * width * hidden + 5 * rows * hidden + 4 * rows * width,
        ),
    )(mask, places, gate, up, *far, *near)


def weight_kernel(mask, tok, cot, *refs):
    far, far_hidden, near = (refs[i * QUARTERS : (i + 1) * QUARTERS] for i in range(3))
    gate_grad, up_grad, down_grad = refs[3 * QUARTERS :]
    f = pl.program_id(0)

    def put(m, out, product):
        @pl.when(mask[m, f] != 0)
        def _():
            out[...] = product().astype(out.dtype)

        @pl.when(mask[m, f] == 0)
        def _():
            out[...] = jnp.zeros_like(out)

    put(0, gate_grad, lambda: dot(tok[...], whole(far, near, 0, 0), (0, 0)))
    put(1, up_grad, lambda: dot(tok[...], whole(far, near, 1, 1), (0, 0)))
    put(2, down_grad, lambda: dot(whole(far_hidden, near, 0, 2), cot[...], (0, 0)))


def weight_gradients(mask, permuted, far, far_hidden, near):
    rows, both = permuted.shape
    width = both // 2
    share, hidden = near[0].shape[1:]
    return pl.pallas_call(
        weight_kernel,
        name="weight_gradients",
        grid_spec=pltpu.PrefetchScalarGridSpec(
            num_scalar_prefetch=1,
            grid=(hidden // BLK,),
            in_specs=[
                pl.BlockSpec((rows, width), lambda f, *_: (0, 0)),
                pl.BlockSpec((rows, width), lambda f, *_: (0, 1)),
            ]
            + [pl.BlockSpec((2, share, BLK), lambda f, *_: (0, 0, f))] * QUARTERS
            + [pl.BlockSpec((1, share, BLK), lambda f, *_: (0, 0, f))] * QUARTERS
            + [pl.BlockSpec((3, share, BLK), lambda f, *_: (0, 0, f))] * QUARTERS,
            out_specs=[
                pl.BlockSpec((width, BLK), lambda f, *_: (0, f)),
                pl.BlockSpec((width, BLK), lambda f, *_: (0, f)),
                pl.BlockSpec((BLK, width), lambda f, *_: (f, 0)),
            ],
        ),
        out_shape=[
            jax.ShapeDtypeStruct((width, hidden), BF16),
            jax.ShapeDtypeStruct((width, hidden), BF16),
            jax.ShapeDtypeStruct((hidden, width), BF16),
        ],
        compiler_params=pltpu.CompilerParams(vmem_limit_bytes=VMEM_LIMIT),
        cost_estimate=pl.CostEstimate(
            flops=6 * rows * width * hidden,
            transcendentals=0,
            bytes_accessed=6 * width * hidden + 6 * rows * hidden,
        ),
    )(mask, permuted, permuted, *far, *far_hidden, *near)


def swiglu(shares):
    gate_value, up_value, hidden_grad = shares[0], shares[1], shares[2]
    sigmoid = jax.nn.sigmoid(gate_value)
    swish = gate_value * sigmoid
    hidden = (swish * up_value).astype(BF16)
    gate_delta = (hidden_grad * up_value * sigmoid * (1.0 + gate_value * (1.0 - sigmoid))).astype(BF16)
    up_delta = (hidden_grad * swish).astype(BF16)
    return jnp.stack([gate_delta, up_delta, hidden])


def reduce_rows(sent, kept, order):
    received = exchange(sent, order[0])
    half = kept.shape[1] // 2
    passed = (kept[:, :half] + received[:, :half].astype(F32)).astype(BF16)
    held = exchange(passed, order[1]).astype(F32) + (kept[:, half:] + received[:, half:].astype(F32))
    for dim in order[2:]:
        half = held.shape[1] // 2
        held = held[:, half:] + exchange(held[:, :half], dim)
    return held


def gather_rows(own, order):
    for dim in reversed(order[1:]):
        own = jnp.concatenate([exchange(own, dim), own], axis=1)
    return own


def layer(tokens, cotangent, gate_weight, up_weight, down_weight, block_mask):
    depth = lax.axis_size("z")
    mine, width = tokens.shape
    mask = block_mask.reshape(3, -1)
    x, y = lax.axis_index("x"), lax.axis_index("y")
    bits = (x ^ (x >> 1)) + 4 * (y ^ (y >> 1))
    other_core = [(0, 1), (1, 0)]

    both = jnp.concatenate([tokens, cotangent], axis=1)
    column = lax.all_to_all(jnp.broadcast_to(both[None], (depth,) + both.shape), "z", 0, 0)
    column = column.reshape(depth * mine, 2 * width)
    gathered = jnp.concatenate([column, lax.ppermute(column, "core", other_core)], axis=0)

    count = gathered.shape[0]
    places = jnp.bitwise_xor(jnp.array(token_places(), jnp.int32), bits)
    source = jnp.repeat(places, GROUP) * GROUP + jnp.tile(jnp.arange(GROUP, dtype=jnp.int32), count // GROUP)
    select = (source[:, None] == jnp.arange(count, dtype=jnp.int32)[None]).astype(BF16)
    permuted = jnp.dot(select, gathered, preferred_element_type=F32).astype(BF16)

    weights = (gate_weight, up_weight, down_weight)
    sent = forward(mask, permuted, 0, *weights, BF16)
    kept = forward(mask, permuted, 1, *weights, F32)

    summed = [reduce_rows(sent[q], kept[q], ORDERS[q]) for q in range(QUARTERS)]
    near = [gather_rows(swiglu(summed[q]), ORDERS[q]) for q in range(QUARTERS)]
    far = [exchange(near[q][:2], ORDERS[q][0]) for q in range(QUARTERS)]
    far_hidden = [exchange(near[q][2:], ORDERS[q][0]) for q in range(QUARTERS)]
    input_grad = input_gradient(mask, places, gate_weight, up_weight, far, near)
    gate_grad, up_grad, down_grad = weight_gradients(mask, permuted, far, far_hidden, near)
    input_grad = input_grad.reshape(2, depth, mine, width)
    input_grad = input_grad[0] + lax.ppermute(input_grad[1], "core", other_core)
    parts = lax.all_to_all(input_grad.astype(BF16), "z", 0, 0)
    input_grad = jnp.sum(parts.astype(F32), axis=0)
    return (input_grad.astype(BF16), gate_grad, up_grad, down_grad)


def solution(mesh):
    torus = Mesh(mesh.devices.reshape(4, 4, -1, 2), ("x", "y", "z", "core"))
    row, col = ("x", "y"), ("z", "core")
    in_specs = (P(col, row), P(col, row), P(row, col), P(row, col), P(col, row), P(None, row, col))
    out_specs = (P(col, row), P(row, col), P(row, col), P(col, row))
    return jax.shard_map(layer, mesh=torus, in_specs=in_specs, out_specs=out_specs, check_vma=False)
```

profile of v0, /device:TPU:14, one launch (start us, length us, event | category | flops | bytes accessed | tf_op | source)
XLA Modules:
  0.0 160.4 jit_solution(5350371778089242743)
XLA Ops:
  1.5 25.9 %all_to_all.10 = bf16[8,32,1024]{2,1,0:T(8,128)(2,1)S(1)} all-to-all(bf16[8,32,1024]{2,1,0:T(8,128)(2,1)S(1)} %broadcast_in_dim.5), channel_id=1, replica_groups=mesh['x'=4,'y'=4,'z'=8,'core'=2] {'z'}, dimensions={0} | all-to-all | bytes 1048576 | tf_op jit(solution)/shard_map/all_to_all | solution.py:258
  29.4 2.0 %convolution_convert_fusion.tok.cot = bf16[512,1024]{1,0:T(8,128)(2,1)S(1)} fusion(bf16[256,1024]{1,0:T(8,128)(2,1)} %collective-permute-done, bf16[256,1024]{1,0:T(8,128)(2,1)} %bitcast.16, s32[512]{0:T(512)S(1)} %add.118), kind=kOutput, calls=%fused_computation | convolution fusion | flops 539754496 | bytes 2099200 | tf_op jit(solution)/shard_map/dot_general | solution.py:266
  33.0 2.8 %shard_map.103 = (bf16[3,64,2048]{2,1,0:T(8,128)(2,1)S(1)}, bf16[3,64,2048]{2,1,0:T(8,128)(2,1)S(1)}, bf16[3,64,2048]{2,1,0:T(8,128)(2,1)S(1)}, bf16[3,64,2048]{2,1,0:T(8,128)(2,1)S(1)}) custom-call(s32[3,4]{1,0:T(4,128)S(1)} %bitcast.10, bf16[512,1024]{1,0:T(8,128)(2,1)S(1)} %convolution_convert_fusion.tok.cot, ...), custom_call_target="tpu_custom_call" | custom-call | flops 1610612736 | bytes 9437184 | tf_op jit(solution)/shard_map/pallas_call | solution.py:86
  35.8 1.7 %collective-permute-start.25 = (bf16[3,64,2048]{2,1,0:T(8,128)(2,1)S(1)}, bf16[3,64,2048]{2,1,0:T(8,128)(2,1)S(1)}, u32[]{:S(2)}, u32[]{:S(2)}) collective-permute-start(bf16[3,64,2048]{2,1,0:T(8,128)(2,1)S(1)} %get-tuple-element.22), channel_id=1, source_target_pairs={{16,32},{32,16},{48,0},{0,48},{17,33},{33,17},{49,1},{1,49},{18,34... | collective-permute-start | bytes 2359304 | tf_op jit(solution)/shard_map/ppermute | solution.py:25
  37.5 2.5 %collective-permute-start.17 = (bf16[3,64,2048]{2,1,0:T(8,128)(2,1)S(1)}, bf16[3,64,2048]{2,1,0:T(8,128)(2,1)S(1)}, u32[]{:S(2)}, u32[]{:S(2)}) collective-permute-start(bf16[3,64,2048]{2,1,0:T(8,128)(2,1)S(1)} %get-tuple-element.20), channel_id=1, source_target_pairs={{0,16},{16,0},{32,48},{48,32},{1,17},{17,1},{33,49},{49,33},{2,18}... | collective-permute-start | bytes 2359304 | tf_op jit(solution)/shard_map/ppermute | solution.py:25
  40.4 3.1 %shard_map.102 = (f32[3,64,2048]{2,1,0:T(8,128)S(1)}, f32[3,64,2048]{2,1,0:T(8,128)S(1)}, f32[3,64,2048]{2,1,0:T(8,128)S(1)}, f32[3,64,2048]{2,1,0:T(8,128)S(1)}) custom-call(s32[3,4]{1,0:T(4,128)S(1)} %bitcast.11, bf16[512,1024]{1,0:T(8,128)(2,1)S(1)} %convolution_convert_fusion.tok.cot, bf16[512,1024]{1,0:T(8,128)(2,1)S(1)} %convolution_convert_fusion.tok.cot, ...), custom_call_target="tpu_custom_call" | custom-call | flops 1610612736 | bytes 12582912 | tf_op jit(solution)/shard_map/pallas_call | solution.py:86
  43.6 11.9 %collective-permute-done.25 = bf16[3,64,2048]{2,1,0:T(8,128)(2,1)S(1)} collective-permute-done((bf16[3,64,2048]{2,1,0:T(8,128)(2,1)S(1)}, bf16[3,64,2048]{2,1,0:T(8,128)(2,1)S(1)}, u32[]{:S(2)}, u32[]{:S(2)}) %collective-permute-start.25) | collective-permute-done | bytes 786464 | tf_op jit(solution)/shard_map/ppermute | solution.py:25
  55.6 2.1 %collective-permute-start.26 = (bf16[3,32,2048]{2,1,0:T(8,128)(2,1)S(1)}, bf16[3,32,2048]{2,1,0:T(8,128)(2,1)S(1)}, u32[]{:S(2)}, u32[]{:S(2)}) collective-permute-start(bf16[3,32,2048]{2,1,0:T(8,128)(2,1)S(1)} %add_convert_fusion), channel_id=1, source_target_pairs={{0,16},{16,0},{32,48},{48,32},{1,17},{17,1},{33,49},{49,33},{2,18}... | collective-permute-start | bytes 1179656 | tf_op jit(solution)/shard_map/ppermute | solution.py:25
  59.4 2.3 %collective-permute-start.10 = (bf16[3,32,2048]{2,1,0:T(8,128)(2,1)S(1)}, bf16[3,32,2048]{2,1,0:T(8,128)(2,1)S(1)}, u32[]{:S(2)}, u32[]{:S(2)}) collective-permute-start(bf16[3,32,2048]{2,1,0:T(8,128)(2,1)S(1)} %add_convert_fusion.2), channel_id=1, source_target_pairs={{0,64},{64,0},{128,192},{192,128},{1,65},{65,1},{129,193},{193,129... | collective-permute-start | bytes 1179656 | tf_op jit(solution)/shard_map/ppermute | solution.py:25
  62.2 3.8 %collective-permute-done.26 = bf16[3,32,2048]{2,1,0:T(8,128)(2,1)S(1)} collective-permute-done((bf16[3,32,2048]{2,1,0:T(8,128)(2,1)S(1)}, bf16[3,32,2048]{2,1,0:T(8,128)(2,1)S(1)}, u32[]{:S(2)}, u32[]{:S(2)}) %collective-permute-start.26) | collective-permute-done | bytes 393248 | tf_op jit(solution)/shard_map/ppermute | solution.py:25
  66.1 2.0 %collective-permute-start.27 = (f32[3,16,2048]{2,1,0:T(8,128)S(1)}, f32[3,16,2048]{2,1,0:T(8,128)S(1)}, u32[]{:S(2)}, u32[]{:S(2)}) collective-permute-start(f32[3,16,2048]{2,1,0:T(8,128)S(1)} %slice.251), channel_id=1, source_target_pairs={{64,128},{128,64},{192,0},{0,192},{65,129},{129,65},{193,1},{1,193... | collective-permute-start | bytes 1179656 | tf_op jit(solution)/shard_map/ppermute | solution.py:25
  68.2 2.7 %collective-permute-start.19 = (f32[3,16,2048]{2,1,0:T(8,128)S(1)}, f32[3,16,2048]{2,1,0:T(8,128)S(1)}, u32[]{:S(2)}, u32[]{:S(2)}) collective-permute-start(f32[3,16,2048]{2,1,0:T(8,128)S(1)} %slice.241), channel_id=1, source_target_pairs={{0,64},{64,0},{128,192},{192,128},{1,65},{65,1},{129,193},{193,129... | collective-permute-start | bytes 1179656 | tf_op jit(solution)/shard_map/ppermute | solution.py:25
  71.1 1.8 %collective-permute-start.11 = (f32[3,16,2048]{2,1,0:T(8,128)S(1)}, f32[3,16,2048]{2,1,0:T(8,128)S(1)}, u32[]{:S(2)}, u32[]{:S(2)}) collective-permute-start(f32[3,16,2048]{2,1,0:T(8,128)S(1)} %slice.231), channel_id=1, source_target_pairs={{16,32},{32,16},{48,0},{0,48},{17,33},{33,17},{49,1},{1,49},{18,34... | collective-permute-start | bytes 1179656 | tf_op jit(solution)/shard_map/ppermute | solution.py:25
  72.9 2.2 %collective-permute-done.2 = bf16[3,32,2048]{2,1,0:T(8,128)(2,1)S(1)} collective-permute-done((bf16[3,32,2048]{2,1,0:T(8,128)(2,1)S(1)}, bf16[3,32,2048]{2,1,0:T(8,128)(2,1)S(1)}, u32[]{:S(2)}, u32[]{:S(2)}) %collective-permute-start.2) | collective-permute-done | bytes 393248 | tf_op jit(solution)/shard_map/ppermute | solution.py:25
  75.9 5.9 %collective-permute-done.27 = f32[3,16,2048]{2,1,0:T(8,128)S(1)} collective-permute-done((f32[3,16,2048]{2,1,0:T(8,128)S(1)}, f32[3,16,2048]{2,1,0:T(8,128)S(1)}, u32[]{:S(2)}, u32[]{:S(2)}) %collective-permute-start.27) | collective-permute-done | bytes 393248 | tf_op jit(solution)/shard_map/ppermute | solution.py:25
  85.9 1.7 %collective-permute-done.28 = f32[3,8,2048]{2,1,0:T(8,128)S(1)} collective-permute-done((f32[3,8,2048]{2,1,0:T(8,128)S(1)}, f32[3,8,2048]{2,1,0:T(8,128)S(1)}, u32[]{:S(2)}, u32[]{:S(2)}) %collective-permute-start.28) | collective-permute-done | bytes 196640 | tf_op jit(solution)/shard_map/ppermute | solution.py:25
  90.9 1.8 %collective-permute-start.5 = (bf16[3,8,2048]{2,1,0:T(8,128)(2,1)S(1)}, bf16[3,8,2048]{2,1,0:T(8,128)(2,1)S(1)}, u32[]{:S(2)}, u32[]{:S(2)}) collective-permute-start(bf16[3,8,2048]{2,1,0:T(8,128)(2,1)S(1)} %pad_maximum_fusion), channel_id=1, source_target_pairs={{16,32},{32,16},{48,0},{0,48},{17,33},{33,17},{49,1},{1,49},{18,34... | collective-permute-start | bytes 294920 | tf_op jit(solution)/shard_map/ppermute | solution.py:25
  92.7 2.1 %collective-permute-start.30 = (bf16[3,16,2048]{2,1,0:T(8,128)(2,1)S(1)}, bf16[3,16,2048]{2,1,0:T(8,128)(2,1)S(1)}, u32[]{:S(2)}, u32[]{:S(2)}) collective-permute-start(bf16[3,16,2048]{2,1,0:T(8,128)(2,1)S(1)} %maximum_maximum_fusion.11), channel_id=1, source_target_pairs={{64,128},{128,64},{192,0},{0,192},{65,129},{129,65},{193,1},{1,193... | collective-permute-start | bytes 589832 | tf_op jit(solution)/shard_map/ppermute | solution.py:25
  96.8 2.6 %collective-permute-start.6 = (bf16[3,16,2048]{2,1,0:T(8,128)(2,1)S(1)}, bf16[3,16,2048]{2,1,0:T(8,128)(2,1)S(1)}, u32[]{:S(2)}, u32[]{:S(2)}) collective-permute-start(bf16[3,16,2048]{2,1,0:T(8,128)(2,1)S(1)} %maximum_maximum_fusion.8), channel_id=1, source_target_pairs={{0,16},{16,0},{32,48},{48,32},{1,17},{17,1},{33,49},{49,33},{2,18}... | collective-permute-start | bytes 589832 | tf_op jit(solution)/shard_map/ppermute | solution.py:25
  100.7 1.8 %collective-permute-done.22 = bf16[3,16,2048]{2,1,0:T(8,128)(2,1)S(1)} collective-permute-done((bf16[3,16,2048]{2,1,0:T(8,128)(2,1)S(1)}, bf16[3,16,2048]{2,1,0:T(8,128)(2,1)S(1)}, u32[]{:S(2)}, u32[]{:S(2)}) %collective-permute-start.22) | collective-permute-done | bytes 196640 | tf_op jit(solution)/shard_map/ppermute | solution.py:25
  103.4 2.6 %collective-permute-start.15 = (bf16[3,32,2048]{2,1,0:T(8,128)(2,1)S(1)}, bf16[3,32,2048]{2,1,0:T(8,128)(2,1)S(1)}, u32[]{:S(2)}, u32[]{:S(2)}) collective-permute-start(bf16[3,32,2048]{2,1,0:T(8,128)(2,1)S(1)} %maximum_maximum_fusion.5), channel_id=1, source_target_pairs={{0,64},{64,0},{128,192},{192,128},{1,65},{65,1},{129,193},{193,129... | collective-permute-start | bytes 1179656 | tf_op jit(solution)/shard_map/ppermute | solution.py:25
  106.6 2.7 %collective-permute-done.31 = bf16[3,32,2048]{2,1,0:T(8,128)(2,1)S(1)} collective-permute-done((bf16[3,32,2048]{2,1,0:T(8,128)(2,1)S(1)}, bf16[3,32,2048]{2,1,0:T(8,128)(2,1)S(1)}, u32[]{:S(2)}, u32[]{:S(2)}) %collective-permute-start.31) | collective-permute-done | bytes 393248 | tf_op jit(solution)/shard_map/ppermute | solution.py:25
  110.3 2.6 %collective-permute-done.23 = bf16[3,32,2048]{2,1,0:T(8,128)(2,1)S(1)} collective-permute-done((bf16[3,32,2048]{2,1,0:T(8,128)(2,1)S(1)}, bf16[3,32,2048]{2,1,0:T(8,128)(2,1)S(1)}, u32[]{:S(2)}, u32[]{:S(2)}) %collective-permute-start.23) | collective-permute-done | bytes 393248 | tf_op jit(solution)/shard_map/ppermute | solution.py:25
  114.6 2.9 %collective-permute-start.16 = (bf16[2,64,2048]{2,1,0:T(8,128)(2,1)S(1)}, bf16[2,64,2048]{2,1,0:T(8,128)(2,1)S(1)}, u32[]{:S(2)}, u32[]{:S(2)}) collective-permute-start(bf16[2,64,2048]{2,1,0:T(8,128)(2,1)S(1)} %slice.237), channel_id=1, source_target_pairs={{64,128},{128,64},{192,0},{0,192},{65,129},{129,65},{193,1},{1,193... | collective-permute-start | bytes 1572872 | tf_op jit(solution)/shard_map/ppermute | solution.py:25
  118.5 3.1 %collective-permute-done.32.refs_3_ = bf16[2,64,2048]{2,1,0:T(8,128)(2,1)S(1)} collective-permute-done((bf16[2,64,2048]{2,1,0:T(8,128)(2,1)S(1)}, bf16[2,64,2048]{2,1,0:T(8,128)(2,1)S(1)}, u32[]{:S(2)}, u32[]{:S(2)}) %collective-permute-start.32) | collective-permute-done | bytes 524320 | tf_op jit(solution)/shard_map/ppermute | solution.py:25
  122.3 4.1 %collective-permute-done.16.refs_1_ = bf16[2,64,2048]{2,1,0:T(8,128)(2,1)S(1)} collective-permute-done((bf16[2,64,2048]{2,1,0:T(8,128)(2,1)S(1)}, bf16[2,64,2048]{2,1,0:T(8,128)(2,1)S(1)}, u32[]{:S(2)}, u32[]{:S(2)}) %collective-permute-start.16) | collective-permute-done | bytes 524320 | tf_op jit(solution)/shard_map/ppermute | solution.py:25
  127.7 2.6 %input_gradient.1 = f32[64,8,512]{2,1,0:T(8,128)S(1)} custom-call(s32[3,4]{1,0:T(4,128)S(1)} %bitcast.12, s32[64]{0:T(128)S(1)} %get-tuple-element.41.places, bf16[512,2048]{1,0:T(8,128)(2,1)S(1)} %copy-done, bf16[512,2048]{1,0:T(8,128)(2,1)S(1)} %copy-done.1, bf16[2,64,2048]{2,1,0:T(8,128)(2,1)S(1)} %collective-permute-done.8.refs_0_, ...), custom_call_target="tpu_custom_call" | custom-call | flops 2147483648 | bytes 10485760 | tf_op jit(solution)/shard_map/input_gradient/pallas_call | solution.py:144
  133.4 5.2 %collective-permute-start.36 = (bf16[1,64,2048]{2,1,0:T(8,128)(2,1)}, bf16[1,64,2048]{2,1,0:T(8,128)(2,1)}, u32[]{:S(2)}, u32[]{:S(2)}) collective-permute-start(bf16[1,64,2048]{2,1,0:T(8,128)(2,1)} %slice.262), channel_id=1, source_target_pairs={{0,16},{16,0},{32,48},{48,32},{1,17},{17,1},{33,49},{49,33},{2,18}... | collective-permute-start | bytes 786440 | tf_op jit(solution)/shard_map/ppermute | solution.py:25
  139.5 4.0 %all-to-all-start.1 = ((bf16[8,32,512]{2,1,0:T(8,128)(2,1)}), bf16[8,32,512]{2,1,0:T(8,128)(2,1)}, u32[]{:S(2)}, u32[]{:S(2)}) async-start(bf16[8,32,512]{2,1,0:T(8,128)(2,1)} %fusion.3), calls=%async_computation.1 | async-start | bytes 524288 | tf_op jit(solution)/shard_map/all_to_all | solution.py:280
  143.6 2.0 %collective-permute-done.36.refs_6_ = bf16[1,64,2048]{2,1,0:T(8,128)(2,1)} collective-permute-done((bf16[1,64,2048]{2,1,0:T(8,128)(2,1)}, bf16[1,64,2048]{2,1,0:T(8,128)(2,1)}, u32[]{:S(2)}, u32[]{:S(2)}) %collective-permute-start.36) | collective-permute-done | bytes 262176 | tf_op jit(solution)/shard_map/ppermute | solution.py:25
  145.5 2.7 %collective-permute-done.35.refs_5_ = bf16[1,64,2048]{2,1,0:T(8,128)(2,1)} collective-permute-done((bf16[1,64,2048]{2,1,0:T(8,128)(2,1)}, bf16[1,64,2048]{2,1,0:T(8,128)(2,1)}, u32[]{:S(2)}, u32[]{:S(2)}) %collective-permute-start.35) | collective-permute-done | bytes 262176 | tf_op jit(solution)/shard_map/ppermute | solution.py:25
  153.6 5.1 %weight_gradients.1 = (bf16[512,2048]{1,0:T(8,128)(2,1)}, bf16[512,2048]{1,0:T(8,128)(2,1)}, bf16[2048,512]{1,0:T(8,128)(2,1)}) custom-call(s32[3,4]{1,0:T(4,128)S(1)} %bitcast.13, bf16[512,1024]{1,0:T(8,128)(2,1)S(1)} %convolution_convert_fusion.tok.cot, bf16[512,1024]{1,0:T(8,128)(2,1)S(1)} %convolution_convert_fusion.tok.cot, ...), custom_call_target="tpu_custom_call" | custom-call | flops 3221225472 | bytes 12582912 | tf_op jit(solution)/shard_map/weight_gradients/pallas_call | solution.py:189
  (159 shorter events, 37.0 us)
Async XLA Ops:
  35.8 19.7 %collective-permute-start.25 = (bf16[3,64,2048]{2,1,0:T(8,128)(2,1)S(1)}, bf16[3,64,2048]{2,1,0:T(8,128)(2,1)S(1)}, u32[]{:S(2)}, u32[]{:S(2)}) collective-permute-start(bf16[3,64,2048]{2,1,0:T(8,128)(2,1)S(1)} %get-tuple-element.22), channel_id=1, source_target_pairs={{16,32},{32,16},{48,0},{0,48},{17,33},{33,17},{49,1},{1,49},{18,34... | collective-permute-start | bytes 2359304 | tf_op jit(solution)/shard_map/ppermute | solution.py:25
  37.5 20.2 %collective-permute-start.17 = (bf16[3,64,2048]{2,1,0:T(8,128)(2,1)S(1)}, bf16[3,64,2048]{2,1,0:T(8,128)(2,1)S(1)}, u32[]{:S(2)}, u32[]{:S(2)}) collective-permute-start(bf16[3,64,2048]{2,1,0:T(8,128)(2,1)S(1)} %get-tuple-element.20), channel_id=1, source_target_pairs={{0,16},{16,0},{32,48},{48,32},{1,17},{17,1},{33,49},{49,33},{2,18}... | collective-permute-start | bytes 2359304 | tf_op jit(solution)/shard_map/ppermute | solution.py:25
  40.0 19.4 %collective-permute-start.9 = (bf16[3,64,2048]{2,1,0:T(8,128)(2,1)S(1)}, bf16[3,64,2048]{2,1,0:T(8,128)(2,1)S(1)}, u32[]{:S(2)}, u32[]{:S(2)}) collective-permute-start(bf16[3,64,2048]{2,1,0:T(8,128)(2,1)S(1)} %get-tuple-element.18), channel_id=1, source_target_pairs={{64,128},{128,64},{192,0},{0,192},{65,129},{129,65},{193,1},{1,193... | collective-permute-start | bytes 2359304 | tf_op jit(solution)/shard_map/ppermute | solution.py:25
  40.4 21.3 %collective-permute-start.1 = (bf16[3,64,2048]{2,1,0:T(8,128)(2,1)S(1)}, bf16[3,64,2048]{2,1,0:T(8,128)(2,1)S(1)}, u32[]{:S(2)}, u32[]{:S(2)}) collective-permute-start(bf16[3,64,2048]{2,1,0:T(8,128)(2,1)S(1)} %get-tuple-element.16), channel_id=1, source_target_pairs={{0,64},{64,0},{128,192},{192,128},{1,65},{65,1},{129,193},{193,129... | collective-permute-start | bytes 2359304 | tf_op jit(solution)/shard_map/ppermute | solution.py:25
  55.6 10.4 %collective-permute-start.26 = (bf16[3,32,2048]{2,1,0:T(8,128)(2,1)S(1)}, bf16[3,32,2048]{2,1,0:T(8,128)(2,1)S(1)}, u32[]{:S(2)}, u32[]{:S(2)}) collective-permute-start(bf16[3,32,2048]{2,1,0:T(8,128)(2,1)S(1)} %add_convert_fusion), channel_id=1, source_target_pairs={{0,16},{16,0},{32,48},{48,32},{1,17},{17,1},{33,49},{49,33},{2,18}... | collective-permute-start | bytes 1179656 | tf_op jit(solution)/shard_map/ppermute | solution.py:25
  57.7 10.3 %collective-permute-start.18 = (bf16[3,32,2048]{2,1,0:T(8,128)(2,1)S(1)}, bf16[3,32,2048]{2,1,0:T(8,128)(2,1)S(1)}, u32[]{:S(2)}, u32[]{:S(2)}) collective-permute-start(bf16[3,32,2048]{2,1,0:T(8,128)(2,1)S(1)} %add_convert_fusion.1), channel_id=1, source_target_pairs={{16,32},{32,16},{48,0},{0,48},{17,33},{33,17},{49,1},{1,49},{18,34... | collective-permute-start | bytes 1179656 | tf_op jit(solution)/shard_map/ppermute | solution.py:25
  59.4 11.5 %collective-permute-start.10 = (bf16[3,32,2048]{2,1,0:T(8,128)(2,1)S(1)}, bf16[3,32,2048]{2,1,0:T(8,128)(2,1)S(1)}, u32[]{:S(2)}, u32[]{:S(2)}) collective-permute-start(bf16[3,32,2048]{2,1,0:T(8,128)(2,1)S(1)} %add_convert_fusion.2), channel_id=1, source_target_pairs={{0,64},{64,0},{128,192},{192,128},{1,65},{65,1},{129,193},{193,129... | collective-permute-start | bytes 1179656 | tf_op jit(solution)/shard_map/ppermute | solution.py:25
  61.8 13.3 %collective-permute-start.2 = (bf16[3,32,2048]{2,1,0:T(8,128)(2,1)S(1)}, bf16[3,32,2048]{2,1,0:T(8,128)(2,1)S(1)}, u32[]{:S(2)}, u32[]{:S(2)}) collective-permute-start(bf16[3,32,2048]{2,1,0:T(8,128)(2,1)S(1)} %add_convert_fusion.3), channel_id=1, source_target_pairs={{64,128},{128,64},{192,0},{0,192},{65,129},{129,65},{193,1},{1,193... | collective-permute-start | bytes 1179656 | tf_op jit(solution)/shard_map/ppermute | solution.py:25
  66.1 15.7 %collective-permute-start.27 = (f32[3,16,2048]{2,1,0:T(8,128)S(1)}, f32[3,16,2048]{2,1,0:T(8,128)S(1)}, u32[]{:S(2)}, u32[]{:S(2)}) collective-permute-start(f32[3,16,2048]{2,1,0:T(8,128)S(1)} %slice.251), channel_id=1, source_target_pairs={{64,128},{128,64},{192,0},{0,192},{65,129},{129,65},{193,1},{1,193... | collective-permute-start | bytes 1179656 | tf_op jit(solution)/shard_map/ppermute | solution.py:25
  68.2 13.8 %collective-permute-start.19 = (f32[3,16,2048]{2,1,0:T(8,128)S(1)}, f32[3,16,2048]{2,1,0:T(8,128)S(1)}, u32[]{:S(2)}, u32[]{:S(2)}) collective-permute-start(f32[3,16,2048]{2,1,0:T(8,128)S(1)} %slice.241), channel_id=1, source_target_pairs={{0,64},{64,0},{128,192},{192,128},{1,65},{65,1},{129,193},{193,129... | collective-permute-start | bytes 1179656 | tf_op jit(solution)/shard_map/ppermute | solution.py:25
  71.1 11.6 %collective-permute-start.11 = (f32[3,16,2048]{2,1,0:T(8,128)S(1)}, f32[3,16,2048]{2,1,0:T(8,128)S(1)}, u32[]{:S(2)}, u32[]{:S(2)}) collective-permute-start(f32[3,16,2048]{2,1,0:T(8,128)S(1)} %slice.231), channel_id=1, source_target_pairs={{16,32},{32,16},{48,0},{0,48},{17,33},{33,17},{49,1},{1,49},{18,34... | collective-permute-start | bytes 1179656 | tf_op jit(solution)/shard_map/ppermute | solution.py:25
  75.2 9.1 %collective-permute-start.3 = (f32[3,16,2048]{2,1,0:T(8,128)S(1)}, f32[3,16,2048]{2,1,0:T(8,128)S(1)}, u32[]{:S(2)}, u32[]{:S(2)}) collective-permute-start(f32[3,16,2048]{2,1,0:T(8,128)S(1)} %slice.221), channel_id=1, source_target_pairs={{0,16},{16,0},{32,48},{48,32},{1,17},{17,1},{33,49},{49,33},{2,18}... | collective-permute-start | bytes 1179656 | tf_op jit(solution)/shard_map/ppermute | solution.py:25
  82.1 7.1 %collective-permute-start.20 = (f32[3,8,2048]{2,1,0:T(8,128)S(1)}, f32[3,8,2048]{2,1,0:T(8,128)S(1)}, u32[]{:S(2)}, u32[]{:S(2)}) collective-permute-start(f32[3,8,2048]{2,1,0:T(8,128)S(1)} %slice.243), channel_id=1, source_target_pairs={{64,128},{128,64},{192,0},{0,192},{65,129},{129,65},{193,1},{1,193... | collective-permute-start | bytes 589832 | tf_op jit(solution)/shard_map/ppermute | solution.py:25
  82.7 7.0 %collective-permute-start.12 = (f32[3,8,2048]{2,1,0:T(8,128)S(1)}, f32[3,8,2048]{2,1,0:T(8,128)S(1)}, u32[]{:S(2)}, u32[]{:S(2)}) collective-permute-start(f32[3,8,2048]{2,1,0:T(8,128)S(1)} %slice.233), channel_id=1, source_target_pairs={{0,16},{16,0},{32,48},{48,32},{1,17},{17,1},{33,49},{49,33},{2,18}... | collective-permute-start | bytes 589832 | tf_op jit(solution)/shard_map/ppermute | solution.py:25
  89.3 6.7 %collective-permute-start.21 = (bf16[3,8,2048]{2,1,0:T(8,128)(2,1)S(1)}, bf16[3,8,2048]{2,1,0:T(8,128)(2,1)S(1)}, u32[]{:S(2)}, u32[]{:S(2)}) collective-permute-start(bf16[3,8,2048]{2,1,0:T(8,128)(2,1)S(1)} %pad_maximum_fusion.2), channel_id=1, source_target_pairs={{64,128},{128,64},{192,0},{0,192},{65,129},{129,65},{193,1},{1,193... | collective-permute-start | bytes 294920 | tf_op jit(solution)/shard_map/ppermute | solution.py:25
  92.7 7.0 %collective-permute-start.30 = (bf16[3,16,2048]{2,1,0:T(8,128)(2,1)S(1)}, bf16[3,16,2048]{2,1,0:T(8,128)(2,1)S(1)}, u32[]{:S(2)}, u32[]{:S(2)}) collective-permute-start(bf16[3,16,2048]{2,1,0:T(8,128)(2,1)S(1)} %maximum_maximum_fusion.11), channel_id=1, source_target_pairs={{64,128},{128,64},{192,0},{0,192},{65,129},{129,65},{193,1},{1,193... | collective-permute-start | bytes 589832 | tf_op jit(solution)/shard_map/ppermute | solution.py:25
  96.1 7.3 %collective-permute-start.14 = (bf16[3,16,2048]{2,1,0:T(8,128)(2,1)S(1)}, bf16[3,16,2048]{2,1,0:T(8,128)(2,1)S(1)}, u32[]{:S(2)}, u32[]{:S(2)}) collective-permute-start(bf16[3,16,2048]{2,1,0:T(8,128)(2,1)S(1)} %maximum_maximum_fusion.9), channel_id=1, source_target_pairs={{16,32},{32,16},{48,0},{0,48},{17,33},{33,17},{49,1},{1,49},{18,34... | collective-permute-start | bytes 589832 | tf_op jit(solution)/shard_map/ppermute | solution.py:25
  96.8 9.2 %collective-permute-start.6 = (bf16[3,16,2048]{2,1,0:T(8,128)(2,1)S(1)}, bf16[3,16,2048]{2,1,0:T(8,128)(2,1)S(1)}, u32[]{:S(2)}, u32[]{:S(2)}) collective-permute-start(bf16[3,16,2048]{2,1,0:T(8,128)(2,1)S(1)} %maximum_maximum_fusion.8), channel_id=1, source_target_pairs={{0,16},{16,0},{32,48},{48,32},{1,17},{17,1},{33,49},{49,33},{2,18}... | collective-permute-start | bytes 589832 | tf_op jit(solution)/shard_map/ppermute | solution.py:25
  99.7 9.6 %collective-permute-start.31 = (bf16[3,32,2048]{2,1,0:T(8,128)(2,1)S(1)}, bf16[3,32,2048]{2,1,0:T(8,128)(2,1)S(1)}, u32[]{:S(2)}, u32[]{:S(2)}) collective-permute-start(bf16[3,32,2048]{2,1,0:T(8,128)(2,1)S(1)} %maximum_maximum_fusion.7), channel_id=1, source_target_pairs={{0,16},{16,0},{32,48},{48,32},{1,17},{17,1},{33,49},{49,33},{2,18}... | collective-permute-start | bytes 1179656 | tf_op jit(solution)/shard_map/ppermute | solution.py:25
  102.5 10.4 %collective-permute-start.23 = (bf16[3,32,2048]{2,1,0:T(8,128)(2,1)S(1)}, bf16[3,32,2048]{2,1,0:T(8,128)(2,1)S(1)}, u32[]{:S(2)}, u32[]{:S(2)}) collective-permute-start(bf16[3,32,2048]{2,1,0:T(8,128)(2,1)S(1)} %maximum_maximum_fusion.6), channel_id=1, source_target_pairs={{16,32},{32,16},{48,0},{0,48},{17,33},{33,17},{49,1},{1,49},{18,34... | collective-permute-start | bytes 1179656 | tf_op jit(solution)/shard_map/ppermute | solution.py:25
  103.4 11.0 %collective-permute-start.15 = (bf16[3,32,2048]{2,1,0:T(8,128)(2,1)S(1)}, bf16[3,32,2048]{2,1,0:T(8,128)(2,1)S(1)}, u32[]{:S(2)}, u32[]{:S(2)}) collective-permute-start(bf16[3,32,2048]{2,1,0:T(8,128)(2,1)S(1)} %maximum_maximum_fusion.5), channel_id=1, source_target_pairs={{0,64},{64,0},{128,192},{192,128},{1,65},{65,1},{129,193},{193,129... | collective-permute-start | bytes 1179656 | tf_op jit(solution)/shard_map/ppermute | solution.py:25
  106.1 12.0 %collective-permute-start.7 = (bf16[3,32,2048]{2,1,0:T(8,128)(2,1)S(1)}, bf16[3,32,2048]{2,1,0:T(8,128)(2,1)S(1)}, u32[]{:S(2)}, u32[]{:S(2)}) collective-permute-start(bf16[3,32,2048]{2,1,0:T(8,128)(2,1)S(1)} %maximum_maximum_fusion.4), channel_id=1, source_target_pairs={{64,128},{128,64},{192,0},{0,192},{65,129},{129,65},{193,1},{1,193... | collective-permute-start | bytes 1179656 | tf_op jit(solution)/shard_map/ppermute | solution.py:25
  109.4 12.2 %collective-permute-start.32 = (bf16[2,64,2048]{2,1,0:T(8,128)(2,1)S(1)}, bf16[2,64,2048]{2,1,0:T(8,128)(2,1)S(1)}, u32[]{:S(2)}, u32[]{:S(2)}) collective-permute-start(bf16[2,64,2048]{2,1,0:T(8,128)(2,1)S(1)} %slice.257), channel_id=1, source_target_pairs={{16,32},{32,16},{48,0},{0,48},{17,33},{33,17},{49,1},{1,49},{18,34... | collective-permute-start | bytes 1572872 | tf_op jit(solution)/shard_map/ppermute | solution.py:25
  113.0 9.3 %collective-permute-start.24 = (bf16[2,64,2048]{2,1,0:T(8,128)(2,1)S(1)}, bf16[2,64,2048]{2,1,0:T(8,128)(2,1)S(1)}, u32[]{:S(2)}, u32[]{:S(2)}) collective-permute-start(bf16[2,64,2048]{2,1,0:T(8,128)(2,1)S(1)} %slice.247), channel_id=1, source_target_pairs={{0,16},{16,0},{32,48},{48,32},{1,17},{17,1},{33,49},{49,33},{2,18}... | collective-permute-start | bytes 1572872 | tf_op jit(solution)/shard_map/ppermute | solution.py:25
  114.6 11.8 %collective-permute-start.16 = (bf16[2,64,2048]{2,1,0:T(8,128)(2,1)S(1)}, bf16[2,64,2048]{2,1,0:T(8,128)(2,1)S(1)}, u32[]{:S(2)}, u32[]{:S(2)}) collective-permute-start(bf16[2,64,2048]{2,1,0:T(8,128)(2,1)S(1)} %slice.237), channel_id=1, source_target_pairs={{64,128},{128,64},{192,0},{0,192},{65,129},{129,65},{193,1},{1,193... | collective-permute-start | bytes 1572872 | tf_op jit(solution)/shard_map/ppermute | solution.py:25
  118.2 9.5 %collective-permute-start.8 = (bf16[2,64,2048]{2,1,0:T(8,128)(2,1)S(1)}, bf16[2,64,2048]{2,1,0:T(8,128)(2,1)S(1)}, u32[]{:S(2)}, u32[]{:S(2)}) collective-permute-start(bf16[2,64,2048]{2,1,0:T(8,128)(2,1)S(1)} %slice.227), channel_id=1, source_target_pairs={{0,64},{64,0},{128,192},{192,128},{1,65},{65,1},{129,193},{193,129... | collective-permute-start | bytes 1572872 | tf_op jit(solution)/shard_map/ppermute | solution.py:25
  130.4 8.4 %collective-permute-start.33 = (f32[8,32,512]{2,1,0:T(8,128)S(1)}, f32[8,32,512]{2,1,0:T(8,128)S(1)}, u32[]{:S(2)}, u32[]{:S(2)}) collective-permute-start(f32[8,32,512]{2,1,0:T(8,128)S(1)} %bitcast.17), channel_id=1, source_target_pairs={{0,1},{1,0},{2,3},{3,2},{4,5},{5,4},{6,7},{7,6},{8,9},{9,8},{10,11... | collective-permute-start | bytes 1572872 | tf_op jit(solution)/shard_map/ppermute | solution.py:279
  133.4 10.2 %collective-permute-start.37 = (bf16[1,64,2048]{2,1,0:T(8,128)(2,1)}, bf16[1,64,2048]{2,1,0:T(8,128)(2,1)S(1)}, u32[]{:S(2)}, u32[]{:S(2)}) collective-permute-start(bf16[1,64,2048]{2,1,0:T(8,128)(2,1)} %slice.263), channel_id=1, source_target_pairs={{16,32},{32,16},{48,0},{0,48},{17,33},{33,17},{49,1},{1,49},{18,34... | collective-permute-start | bytes 786440 | tf_op jit(solution)/shard_map/ppermute | solution.py:25
  133.4 12.2 %collective-permute-start.36 = (bf16[1,64,2048]{2,1,0:T(8,128)(2,1)}, bf16[1,64,2048]{2,1,0:T(8,128)(2,1)}, u32[]{:S(2)}, u32[]{:S(2)}) collective-permute-start(bf16[1,64,2048]{2,1,0:T(8,128)(2,1)} %slice.262), channel_id=1, source_target_pairs={{0,16},{16,0},{32,48},{48,32},{1,17},{17,1},{33,49},{49,33},{2,18}... | collective-permute-start | bytes 786440 | tf_op jit(solution)/shard_map/ppermute | solution.py:25
  138.5 9.7 %collective-permute-start.35 = (bf16[1,64,2048]{2,1,0:T(8,128)(2,1)}, bf16[1,64,2048]{2,1,0:T(8,128)(2,1)}, u32[]{:S(2)}, u32[]{:S(2)}) collective-permute-start(bf16[1,64,2048]{2,1,0:T(8,128)(2,1)} %slice.261), channel_id=1, source_target_pairs={{64,128},{128,64},{192,0},{0,192},{65,129},{129,65},{193,1},{1,193... | collective-permute-start | bytes 786440 | tf_op jit(solution)/shard_map/ppermute | solution.py:25
  138.7 9.5 %collective-permute-start.34 = (bf16[1,64,2048]{2,1,0:T(8,128)(2,1)}, bf16[1,64,2048]{2,1,0:T(8,128)(2,1)}, u32[]{:S(2)}, u32[]{:S(2)}) collective-permute-start(bf16[1,64,2048]{2,1,0:T(8,128)(2,1)} %slice.260), channel_id=1, source_target_pairs={{0,64},{64,0},{128,192},{192,128},{1,65},{65,1},{129,193},{193,129... | collective-permute-start | bytes 786440 | tf_op jit(solution)/shard_map/ppermute | solution.py:25
  139.5 19.3 %all-to-all-start.1 = ((bf16[8,32,512]{2,1,0:T(8,128)(2,1)}), bf16[8,32,512]{2,1,0:T(8,128)(2,1)}, u32[]{:S(2)}, u32[]{:S(2)}) async-start(bf16[8,32,512]{2,1,0:T(8,128)(2,1)} %fusion.3), calls=%async_computation.1 | async-start | bytes 524288 | tf_op jit(solution)/shard_map/all_to_all | solution.py:280
  (30 other events, 283.2 us)
where the time goes:
time: 163 us; the launch traced here: 160 us
  waiting for transfers between devices  51.8 us (32%)
  starting transfers between devices  50 us (31%)
  blocking collectives  25.9 us (16%)
  Pallas kernels  13.6 us (8%)
  local copies, waits for them, and re-layouts  11 us (7%)
  other arithmetic  4.89 us (3%)
  matrix products  1.95 us (1%)
    ppermute x36, waiting for transfers between devices, exchange(): return lax.ppermute(value, axis, pairs)  50.5 us
    ppermute x36, starting transfers between devices, exchange(): return lax.ppermute(value, axis, pairs)  45.9 us
    all_to_all x1, blocking collectives, layer(): lax.all_to_all(jnp.broadcast_to(both[None], (depth,) + both.shape), 'z',...  25.9 us
    unnamed x47, local copies, waits for them, and re-layouts  7.63 us
    pallas_call x2, Pallas kernels, forward(): pl.pallas_call(forward_kernel, grid_spec=pltpu.PrefetchScalarGridSpec(num...  5.89 us
    pallas_call x1, Pallas kernels, weight_gradients(): pl.pallas_call(weight_kernel, name='weight_gradients', grid_spec=pltpu.Pr...  5.13 us
    all_to_all x1, starting transfers between devices, layer(): parts = lax.all_to_all(input_grad.astype(BF16), 'z', 0, 0)  4.04 us
  transfers between devices with their start and end apart: 39, of which 20 were waited for; matrix products, arithmetic and copies ran while one was open for 4% of the time, Pallas kernels for 5%

commit v1 on v0

--- a/solution.py
+++ b/solution.py
@@ -11,18 +11,23 @@
 F32 = jnp.float32
 BF16 = jnp.bfloat16
 
-PAIRS_LOW = [(0, 1), (1, 0), (2, 3), (3, 2)]
-PAIRS_HIGH = [(1, 2), (2, 1), (3, 0), (0, 3)]
-DIMS = (("x", PAIRS_LOW), ("x", PAIRS_HIGH), ("y", PAIRS_LOW), ("y", PAIRS_HIGH))
-ORDERS = ((0, 1, 2, 3), (1, 0, 3, 2), (2, 3, 0, 1), (3, 2, 1, 0))
-QUARTERS = len(ORDERS)
+FLIP = ((1, 0, 3, 2), (3, 2, 1, 0))
+ORDERS = (((0, 1, 2, 3), (1, 0, 3, 2)), ((2, 3, 0, 1), (3, 2, 1, 0)))
+CHAINS = 2
+PIECES = 4
 NODES = 16
-GROUP = 8
-
-
-def exchange(value, dim):
-    axis, pairs = DIMS[dim]
-    return lax.ppermute(value, axis, pairs)
+GROUP = 16
+
+
+def exchange(value, chain, step):
+    pairs = []
+    for x in range(4):
+        for y in range(4):
+            for core in range(2):
+                dim = ORDERS[core][chain][step]
+                to_x, to_y = (FLIP[dim][x], y) if dim < 2 else (x, FLIP[dim - 2][y])
+                pairs.append((x * 8 + y * 2 + core, to_x * 8 + to_y * 2 + core))
+    return lax.ppermute(value, ("x", "y", "core"), pairs)
 
 
 def block_order(order):
@@ -33,11 +38,11 @@
     return kept
 
 
-def token_places():
+def token_places(core):
     half = NODES // 2
-    orders = [block_order(order) for order in ORDERS]
-    places = [q * NODES + p for q in range(QUARTERS) for p in orders[q][:half]]
-    places += [q * NODES + p for q in range(QUARTERS) for p in orders[q][half:]]
+    orders = [block_order(order) for order in ORDERS[core]]
+    places = [chain * NODES + p for chain in range(CHAINS) for p in orders[chain][:half]]
+    places += [chain * NODES + p for chain in range(CHAINS) for p in orders[chain][half:]]
     return places
 
 
@@ -46,8 +51,8 @@
 
 
 def forward_kernel(mask, tok, cot, gate, up, down, *refs):
-    outs = refs[:QUARTERS]
-    buffers, sems = refs[QUARTERS:-1], refs[-1]
+    outs = refs[:PIECES]
+    buffers, sems = refs[PIECES:-1], refs[-1]
     f = pl.program_id(0)
     rows = outs[0].shape[1]
 
@@ -82,7 +87,7 @@
     rows, width = count // 2, both // 2
     hidden = gate.shape[1]
     blocks = hidden // BLK
-    share = rows // QUARTERS
+    share = rows // PIECES
     return pl.pallas_call(
         forward_kernel,
         grid_spec=pltpu.PrefetchScalarGridSpec(
@@ -93,7 +98,7 @@
                 pl.BlockSpec((rows, width), lambda f, mask: (half, 1)),
             ]
             + [pl.BlockSpec(memory_space=pl.ANY)] * 3,
-            out_specs=[pl.BlockSpec((3, share, BLK), lambda f, mask: (0, 0, f))] * QUARTERS,
+            out_specs=[pl.BlockSpec((3, share, BLK), lambda f, mask: (0, 0, f))] * PIECES,
             scratch_shapes=[
                 pltpu.VMEM((blocks, width, BLK), BF16),
                 pltpu.VMEM((blocks, width, BLK), BF16),
@@ -101,7 +106,7 @@
                 pltpu.SemaphoreType.DMA((3, blocks)),
             ],
         ),
-        out_shape=[jax.ShapeDtypeStruct((3, share, hidden), dtype)] * QUARTERS,
+        out_shape=[jax.ShapeDtypeStruct((3, share, hidden), dtype)] * PIECES,
         compiler_params=pltpu.CompilerParams(vmem_limit_bytes=VMEM_LIMIT),
         cost_estimate=pl.CostEstimate(
             flops=6 * rows * width * hidden,
@@ -116,8 +121,8 @@
 
 
 def input_kernel(mask, places, gate, up, *refs):
-    far, near = refs[:QUARTERS], refs[QUARTERS : 2 * QUARTERS]
-    input_grad, acc = refs[2 * QUARTERS :]
+    far, near = refs[:PIECES], refs[PIECES : 2 * PIECES]
+    input_grad, acc = refs[2 * PIECES :]
     f = pl.program_id(0)
 
     @pl.when(f == 0)
@@ -139,7 +144,7 @@
 def input_gradient(mask, places, gate, up, far, near):
     width, hidden = gate.shape
     share = near[0].shape[1]
-    rows = 2 * QUARTERS * share
+    rows = 2 * PIECES * share
     groups = rows // GROUP
     return pl.pallas_call(
         input_kernel,
@@ -148,8 +153,8 @@
             num_scalar_prefetch=2,
             grid=(hidden // BLK,),
             in_specs=[pl.BlockSpec((width, BLK), lambda f, *_: (0, f))] * 2
-            + [pl.BlockSpec((2, share, BLK), lambda f, *_: (0, 0, f))] * QUARTERS
-            + [pl.BlockSpec((3, share, BLK), lambda f, *_: (0, 0, f))] * QUARTERS,
+            + [pl.BlockSpec((2, share, BLK), lambda f, *_: (0, 0, f))] * PIECES
+            + [pl.BlockSpec((3, share, BLK), lambda f, *_: (0, 0, f))] * PIECES,
             out_specs=pl.BlockSpec((groups, GROUP, width), lambda f, *_: (0, 0, 0)),
             scratch_shapes=[pltpu.VMEM((rows, width), F32)],
         ),
@@ -164,8 +169,8 @@
 
 
 def weight_kernel(mask, tok, cot, *refs):
-    far, far_hidden, near = (refs[i * QUARTERS : (i + 1) * QUARTERS] for i in range(3))
-    gate_grad, up_grad, down_grad = refs[3 * QUARTERS :]
+    far, far_hidden, near = (refs[i * PIECES : (i + 1) * PIECES] for i in range(3))
+    gate_grad, up_grad, down_grad = refs[3 * PIECES :]
     f = pl.program_id(0)
 
     def put(m, out, product):
@@ -196,9 +201,9 @@
                 pl.BlockSpec((rows, width), lambda f, *_: (0, 0)),
                 pl.BlockSpec((rows, width), lambda f, *_: (0, 1)),
             ]
-            + [pl.BlockSpec((2, share, BLK), lambda f, *_: (0, 0, f))] * QUARTERS
-            + [pl.BlockSpec((1, share, BLK), lambda f, *_: (0, 0, f))] * QUARTERS
-            + [pl.BlockSpec((3, share, BLK), lambda f, *_: (0, 0, f))] * QUARTERS,
+            + [pl.BlockSpec((2, share, BLK), lambda f, *_: (0, 0, f))] * PIECES
+            + [pl.BlockSpec((1, share, BLK), lambda f, *_: (0, 0, f))] * PIECES
+            + [pl.BlockSpec((3, share, BLK), lambda f, *_: (0, 0, f))] * PIECES,
             out_specs=[
                 pl.BlockSpec((width, BLK), lambda f, *_: (0, f)),
                 pl.BlockSpec((width, BLK), lambda f, *_: (0, f)),
@@ -229,21 +234,33 @@
     return jnp.stack([gate_delta, up_delta, hidden])
 
 
-def reduce_rows(sent, kept, order):
-    received = exchange(sent, order[0])
-    half = kept.shape[1] // 2
-    passed = (kept[:, :half] + received[:, :half].astype(F32)).astype(BF16)
-    held = exchange(passed, order[1]).astype(F32) + (kept[:, half:] + received[:, half:].astype(F32))
-    for dim in order[2:]:
-        half = held.shape[1] // 2
-        held = held[:, half:] + exchange(held[:, :half], dim)
-    return held
-
-
-def gather_rows(own, order):
-    for dim in reversed(order[1:]):
-        own = jnp.concatenate([exchange(own, dim), own], axis=1)
-    return own
+def reduce_rows(sent, kept):
+    chains = range(CHAINS)
+    ahead = [exchange(sent[2 * c], c, 0) for c in chains]
+    rest = [exchange(sent[2 * c + 1], c, 0) for c in chains]
+    half = ahead[0].shape[1] // 2
+    quarter = half // 2
+    passed = [(kept[2 * c] + ahead[c].astype(F32)).astype(BF16) for c in chains]
+    ahead = [exchange(passed[c][:, :half], c, 1) for c in chains]
+    last = [exchange(passed[c][:, half:], c, 1) for c in chains]
+    summed = []
+    for c in chains:
+        own, got = kept[2 * c + 1], rest[c]
+        third = own[:, :half] + got[:, :half].astype(F32) + ahead[c].astype(F32)
+        held = own[:, half:] + got[:, half:].astype(F32) + last[c].astype(F32)
+        held = held + exchange(third, c, 2)
+        summed.append(held[:, quarter:] + exchange(held[:, :quarter], c, 3))
+    return summed
+
+
+def gather_rows(own):
+    near = []
+    for c in range(CHAINS):
+        rows = own[c]
+        for step in (3, 2):
+            rows = jnp.concatenate([exchange(rows, c, step), rows], axis=1)
+        near += [exchange(rows, c, 1), rows]
+    return near
 
 
 def layer(tokens, cotangent, gate_weight, up_weight, down_weight, block_mask):
@@ -260,7 +277,8 @@
     gathered = jnp.concatenate([column, lax.ppermute(column, "core", other_core)], axis=0)
 
     count = gathered.shape[0]
-    places = jnp.bitwise_xor(jnp.array(token_places(), jnp.int32), bits)
+    core = lax.axis_index("core")
+    places = jnp.where(core == 0, *(jnp.array(token_places(c), jnp.int32) for c in range(2))) ^ bits
     source = jnp.repeat(places, GROUP) * GROUP + jnp.tile(jnp.arange(GROUP, dtype=jnp.int32), count // GROUP)
     select = (source[:, None] == jnp.arange(count, dtype=jnp.int32)[None]).astype(BF16)
     permuted = jnp.dot(select, gathered, preferred_element_type=F32).astype(BF16)
@@ -269,10 +287,11 @@
     sent = forward(mask, permuted, 0, *weights, BF16)
     kept = forward(mask, permuted, 1, *weights, F32)
 
-    summed = [reduce_rows(sent[q], kept[q], ORDERS[q]) for q in range(QUARTERS)]
-    near = [gather_rows(swiglu(summed[q]), ORDERS[q]) for q in range(QUARTERS)]
-    far = [exchange(near[q][:2], ORDERS[q][0]) for q in range(QUARTERS)]
-    far_hidden = [exchange(near[q][2:], ORDERS[q][0]) for q in range(QUARTERS)]
+    near = gather_rows([swiglu(shares) for shares in reduce_rows(sent, kept)])
+    rest = [exchange(near[2 * c + 1][:2], c, 0) for c in range(CHAINS)]
+    ahead = [exchange(near[2 * c][:2], c, 0) for c in range(CHAINS)]
+    far = [piece for c in range(CHAINS) for piece in (ahead[c], rest[c])]
+    far_hidden = [exchange(near[i][2:], i // 2, 0) for i in range(PIECES)]
     input_grad = input_gradient(mask, places, gate_weight, up_weight, far, near)
     gate_grad, up_grad, down_grad = weight_gradients(mask, permuted, far, far_hidden, near)
     input_grad = input_grad.reshape(2, depth, mine, width)

time: 163 us -> 167 us (1.025)
  the two profiles are of different devices: /device:TPU:14 before, /device:TPU:1 now
where the time goes in v1:
time: 167 us; the launch traced here: 166 us
  waiting for transfers between devices  63.5 us (38%)
  starting transfers between devices  45.2 us (27%)
  blocking collectives  25.2 us (15%)
  Pallas kernels  13.9 us (8%)
  local copies, waits for them, and re-layouts  10.5 us (6%)
  other arithmetic  4.66 us (3%)
  matrix products  1.95 us (1%)
    ppermute x26, waiting for transfers between devices, exchange(): return lax.ppermute(value, ('x', 'y', 'core'), pairs)  61.8 us
    ppermute x26, starting transfers between devices, exchange(): return lax.ppermute(value, ('x', 'y', 'core'), pairs)  27.8 us
    all_to_all x1, blocking collectives, layer(): lax.all_to_all(jnp.broadcast_to(both[None], (depth,) + both.shape), 'z',...  25.2 us
    ppermute x1, starting transfers between devices, layer(): input_grad = input_grad[0] + lax.ppermute(input_grad[1], 'core', other_core)  11 us
    unnamed x47, local copies, waits for them, and re-layouts  7.05 us
    pallas_call x1, Pallas kernels, weight_gradients(): pl.pallas_call(weight_kernel, name='weight_gradients', grid_spec=pltpu.Pr...  5.9 us
    pallas_call x2, Pallas kernels, forward(): pl.pallas_call(forward_kernel, grid_spec=pltpu.PrefetchScalarGridSpec(num...  5.86 us
    all_to_all x1, starting transfers between devices, layer(): parts = lax.all_to_all(input_grad.astype(BF16), 'z', 0, 0)  4.04 us
  transfers between devices with their start and end apart: 29, of which 21 were waited for; matrix products, arithmetic and copies ran while one was open for 3% of the time, Pallas kernels for 5%

profile of v1, /device:TPU:1, one launch (start us, length us, event | category | flops | bytes accessed | tf_op | source)
XLA Modules:
  0.0 165.8 jit_solution(6304489698772508799)
XLA Ops:
  1.5 25.2 %all_to_all.10 = bf16[8,32,1024]{2,1,0:T(8,128)(2,1)} all-to-all(bf16[8,32,1024]{2,1,0:T(8,128)(2,1)S(1)} %broadcast_in_dim.5), channel_id=1, replica_groups=mesh['x'=4,'y'=4,'z'=8,'core'=2] {'z'}, dimensions={0} | all-to-all | bytes 1048576 | tf_op jit(solution)/shard_map/all_to_all | solution.py:275
  26.7 2.3 %collective-permute-start = (bf16[256,1024]{1,0:T(8,128)(2,1)}, bf16[256,1024]{1,0:T(8,128)(2,1)}, u32[]{:S(2)}, u32[]{:S(2)}) collective-permute-start(bf16[256,1024]{1,0:T(8,128)(2,1)} %bitcast), channel_id=1, source_target_pairs={{0,1},{1,0},{2,3},{3,2},{4,5},{5,4},{6,7},{7,6},{8,9},{9,8},{10,11... | collective-permute-start | bytes 1572872 | tf_op jit(solution)/shard_map/ppermute | solution.py:277
  29.2 1.7 %collective-permute-done = bf16[256,1024]{1,0:T(8,128)(2,1)} collective-permute-done((bf16[256,1024]{1,0:T(8,128)(2,1)}, bf16[256,1024]{1,0:T(8,128)(2,1)}, u32[]{:S(2)}, u32[]{:S(2)}) %collective-permute-start) | collective-permute-done | bytes 524320 | tf_op jit(solution)/shard_map/ppermute | solution.py:277
  30.9 2.0 %convolution_convert_fusion.tok.cot = bf16[512,1024]{1,0:T(8,128)(2,1)S(1)} fusion(bf16[256,1024]{1,0:T(8,128)(2,1)} %collective-permute-done, bf16[256,1024]{1,0:T(8,128)(2,1)} %bitcast, s32[512]{0:T(512)S(1)} %add.80), kind=kOutput, calls=%fused_computation.2 | convolution fusion | flops 539754496 | bytes 2099200 | tf_op jit(solution)/shard_map/dot_general | solution.py:284
  34.5 2.8 %shard_map.112 = (bf16[3,64,2048]{2,1,0:T(8,128)(2,1)S(1)}, bf16[3,64,2048]{2,1,0:T(8,128)(2,1)S(1)}, bf16[3,64,2048]{2,1,0:T(8,128)(2,1)S(1)}, bf16[3,64,2048]{2,1,0:T(8,128)(2,1)S(1)}) custom-call(s32[3,4]{1,0:T(4,128)S(1)} %bitcast.10, bf16[512,1024]{1,0:T(8,128)(2,1)S(1)} %convolution_convert_fusion.tok.cot, ...), custom_call_target="tpu_custom_call" | custom-call | flops 1610612736 | bytes 9437184 | tf_op jit(solution)/shard_map/pallas_call | solution.py:91
  37.2 3.4 %collective-permute-start.13 = (bf16[3,64,2048]{2,1,0:T(8,128)(2,1)S(1)}, bf16[3,64,2048]{2,1,0:T(8,128)(2,1)S(1)}, u32[]{:S(2)}, u32[]{:S(2)}) collective-permute-start(bf16[3,64,2048]{2,1,0:T(8,128)(2,1)S(1)} %get-tuple-element.22), channel_id=1, source_target_pairs={{0,192},{1,49},{16,208},{17,33},{32,224},{33,17},{48,240},{49,1},{... | collective-permute-start | bytes 2359304 | tf_op jit(solution)/shard_map/ppermute | solution.py:30
  42.2 3.1 %shard_map.111 = (f32[3,64,2048]{2,1,0:T(8,128)S(1)}, f32[3,64,2048]{2,1,0:T(8,128)S(1)}, f32[3,64,2048]{2,1,0:T(8,128)S(1)}, f32[3,64,2048]{2,1,0:T(8,128)S(1)}) custom-call(s32[3,4]{1,0:T(4,128)S(1)} %bitcast.11, bf16[512,1024]{1,0:T(8,128)(2,1)S(1)} %convolution_convert_fusion.tok.cot, bf16[512,1024]{1,0:T(8,128)(2,1)S(1)} %convolution_convert_fusion.tok.cot, ...), custom_call_target="tpu_custom_call" | custom-call | flops 1610612736 | bytes 12582912 | tf_op jit(solution)/shard_map/pallas_call | solution.py:91
  45.3 5.0 %collective-permute-done.13 = bf16[3,64,2048]{2,1,0:T(8,128)(2,1)S(1)} collective-permute-done((bf16[3,64,2048]{2,1,0:T(8,128)(2,1)S(1)}, bf16[3,64,2048]{2,1,0:T(8,128)(2,1)S(1)}, u32[]{:S(2)}, u32[]{:S(2)}) %collective-permute-start.13) | collective-permute-done | bytes 786464 | tf_op jit(solution)/shard_map/ppermute | solution.py:30
  52.1 2.7 %collective-permute-start.4 = (bf16[3,32,2048]{2,1,0:T(8,128)(2,1)S(1)}, bf16[3,32,2048]{2,1,0:T(8,128)(2,1)S(1)}, u32[]{:S(2)}, u32[]{:S(2)}) collective-permute-start(bf16[3,32,2048]{2,1,0:T(8,128)(2,1)S(1)} %get-tuple-element.33), channel_id=1, source_target_pairs={{0,192},{1,49},{16,208},{17,33},{32,224},{33,17},{48,240},{49,1},{... | collective-permute-start | bytes 1179656 | tf_op jit(solution)/shard_map/ppermute | solution.py:30
  54.8 3.9 %collective-permute-done.12 = bf16[3,64,2048]{2,1,0:T(8,128)(2,1)S(1)} collective-permute-done((bf16[3,64,2048]{2,1,0:T(8,128)(2,1)S(1)}, bf16[3,64,2048]{2,1,0:T(8,128)(2,1)S(1)}, u32[]{:S(2)}, u32[]{:S(2)}) %collective-permute-start.12) | collective-permute-done | bytes 786464 | tf_op jit(solution)/shard_map/ppermute | solution.py:30
  58.7 5.8 %collective-permute-done.15 = bf16[3,32,2048]{2,1,0:T(8,128)(2,1)S(1)} collective-permute-done((bf16[3,32,2048]{2,1,0:T(8,128)(2,1)S(1)}, bf16[3,32,2048]{2,1,0:T(8,128)(2,1)S(1)}, u32[]{:S(2)}, u32[]{:S(2)}) %collective-permute-start.15) | collective-permute-done | bytes 393248 | tf_op jit(solution)/shard_map/ppermute | solution.py:30
  64.6 2.2 %collective-permute-start.16 = (f32[3,32,2048]{2,1,0:T(8,128)S(1)}, f32[3,32,2048]{2,1,0:T(8,128)S(1)}, u32[]{:S(2)}, u32[]{:S(2)}) collective-permute-start(f32[3,32,2048]{2,1,0:T(8,128)S(1)} %convert_add_fusion), channel_id=1, source_target_pairs={{0,48},{1,193},{16,32},{17,209},{32,16},{33,225},{48,0},{49,241},{... | collective-permute-start | bytes 2359304 | tf_op jit(solution)/shard_map/ppermute | solution.py:30
  67.6 2.6 %collective-permute-start.3 = (bf16[3,32,2048]{2,1,0:T(8,128)(2,1)S(1)}, bf16[3,32,2048]{2,1,0:T(8,128)(2,1)S(1)}, u32[]{:S(2)}, u32[]{:S(2)}) collective-permute-start(bf16[3,32,2048]{2,1,0:T(8,128)(2,1)S(1)} %get-tuple-element.32), channel_id=1, source_target_pairs={{0,192},{1,49},{16,208},{17,33},{32,224},{33,17},{48,240},{49,1},{... | collective-permute-start | bytes 1179656 | tf_op jit(solution)/shard_map/ppermute | solution.py:30
  70.2 4.4 %collective-permute-done.14 = bf16[3,32,2048]{2,1,0:T(8,128)(2,1)S(1)} collective-permute-done((bf16[3,32,2048]{2,1,0:T(8,128)(2,1)S(1)}, bf16[3,32,2048]{2,1,0:T(8,128)(2,1)S(1)}, u32[]{:S(2)}, u32[]{:S(2)}) %collective-permute-start.14) | collective-permute-done | bytes 393248 | tf_op jit(solution)/shard_map/ppermute | solution.py:30
  74.7 4.7 %collective-permute-done.16 = f32[3,32,2048]{2,1,0:T(8,128)S(1)} collective-permute-done((f32[3,32,2048]{2,1,0:T(8,128)S(1)}, f32[3,32,2048]{2,1,0:T(8,128)S(1)}, u32[]{:S(2)}, u32[]{:S(2)}) %collective-permute-start.16) | collective-permute-done | bytes 786464 | tf_op jit(solution)/shard_map/ppermute | solution.py:30
  80.0 2.3 %collective-permute-done.5 = f32[3,32,2048]{2,1,0:T(8,128)S(1)} collective-permute-done((f32[3,32,2048]{2,1,0:T(8,128)S(1)}, f32[3,32,2048]{2,1,0:T(8,128)S(1)}, u32[]{:S(2)}, u32[]{:S(2)}) %collective-permute-start.5) | collective-permute-done | bytes 786464 | tf_op jit(solution)/shard_map/ppermute | solution.py:30
  82.7 3.6 %collective-permute-done.17 = f32[3,16,2048]{2,1,0:T(8,128)S(1)} collective-permute-done((f32[3,16,2048]{2,1,0:T(8,128)S(1)}, f32[3,16,2048]{2,1,0:T(8,128)S(1)}, u32[]{:S(2)}, u32[]{:S(2)}) %collective-permute-start.17) | collective-permute-done | bytes 393248 | tf_op jit(solution)/shard_map/ppermute | solution.py:30
  87.6 3.1 %collective-permute-done.6 = f32[3,16,2048]{2,1,0:T(8,128)S(1)} collective-permute-done((f32[3,16,2048]{2,1,0:T(8,128)S(1)}, f32[3,16,2048]{2,1,0:T(8,128)S(1)}, u32[]{:S(2)}, u32[]{:S(2)}) %collective-permute-start.6) | collective-permute-done | bytes 393248 | tf_op jit(solution)/shard_map/ppermute | solution.py:30
  91.6 2.7 %collective-permute-start.19 = (bf16[3,32,2048]{2,1,0:T(8,128)(2,1)S(1)}, bf16[3,32,2048]{2,1,0:T(8,128)(2,1)S(1)}, u32[]{:S(2)}, u32[]{:S(2)}) collective-permute-start(bf16[3,32,2048]{2,1,0:T(8,128)(2,1)S(1)} %maximum_maximum_fusion.3), channel_id=1, source_target_pairs={{0,48},{1,193},{16,32},{17,209},{32,16},{33,225},{48,0},{49,241},{... | collective-permute-start | bytes 1179656 | tf_op jit(solution)/shard_map/ppermute | solution.py:30
  94.3 2.5 %collective-permute-done.7 = bf16[3,16,2048]{2,1,0:T(8,128)(2,1)S(1)} collective-permute-done((bf16[3,16,2048]{2,1,0:T(8,128)(2,1)S(1)}, bf16[3,16,2048]{2,1,0:T(8,128)(2,1)S(1)}, u32[]{:S(2)}, u32[]{:S(2)}) %collective-permute-start.7) | collective-permute-done | bytes 196640 | tf_op jit(solution)/shard_map/ppermute | solution.py:30
  96.9 4.1 %collective-permute-done.19 = bf16[3,32,2048]{2,1,0:T(8,128)(2,1)S(1)} collective-permute-done((bf16[3,32,2048]{2,1,0:T(8,128)(2,1)S(1)}, bf16[3,32,2048]{2,1,0:T(8,128)(2,1)S(1)}, u32[]{:S(2)}, u32[]{:S(2)}) %collective-permute-start.19) | collective-permute-done | bytes 393248 | tf_op jit(solution)/shard_map/ppermute | solution.py:30
  102.0 1.8 %collective-permute-done.8 = bf16[3,32,2048]{2,1,0:T(8,128)(2,1)S(1)} collective-permute-done((bf16[3,32,2048]{2,1,0:T(8,128)(2,1)S(1)}, bf16[3,32,2048]{2,1,0:T(8,128)(2,1)S(1)}, u32[]{:S(2)}, u32[]{:S(2)}) %collective-permute-start.8) | collective-permute-done | bytes 393248 | tf_op jit(solution)/shard_map/ppermute | solution.py:30
  103.9 1.9 %collective-permute-start.9 = (bf16[3,64,2048]{2,1,0:T(8,128)(2,1)S(1)}, bf16[3,64,2048]{2,1,0:T(8,128)(2,1)S(1)}, u32[]{:S(2)}, u32[]{:S(2)}) collective-permute-start(bf16[3,64,2048]{2,1,0:T(8,128)(2,1)S(1)} %maximum_maximum_fusion.refs_5_.refs_9_), channel_id=1, source_target_pairs={{0,192},{1,49},{16,208},{17,33},{32,224},{33,17},{48,240},{49,1},{... | collective-permute-start | bytes 2359304 | tf_op jit(solution)/shard_map/ppermute | solution.py:30
  106.8 9.7 %collective-permute-done.20.refs_6_.refs_10_ = bf16[3,64,2048]{2,1,0:T(8,128)(2,1)S(1)} collective-permute-done((bf16[3,64,2048]{2,1,0:T(8,128)(2,1)S(1)}, bf16[3,64,2048]{2,1,0:T(8,128)(2,1)S(1)}, u32[]{:S(2)}, u32[]{:S(2)}) %collective-permute-start.20) | collective-permute-done | bytes 786464 | tf_op jit(solution)/shard_map/ppermute | solution.py:30
  116.5 2.7 %collective-permute-start.21 = (bf16[2,64,2048]{2,1,0:T(8,128)(2,1)S(1)}, bf16[2,64,2048]{2,1,0:T(8,128)(2,1)S(1)}, u32[]{:S(2)}, u32[]{:S(2)}) collective-permute-start(bf16[2,64,2048]{2,1,0:T(8,128)(2,1)S(1)} %slice.150), channel_id=1, source_target_pairs={{0,192},{1,49},{16,208},{17,33},{32,224},{33,17},{48,240},{49,1},{... | collective-permute-start | bytes 1572872 | tf_op jit(solution)/shard_map/ppermute | solution.py:30
  119.4 2.5 %collective-permute-done.22.refs_3_ = bf16[2,64,2048]{2,1,0:T(8,128)(2,1)S(1)} collective-permute-done((bf16[2,64,2048]{2,1,0:T(8,128)(2,1)S(1)}, bf16[2,64,2048]{2,1,0:T(8,128)(2,1)S(1)}, u32[]{:S(2)}, u32[]{:S(2)}) %collective-permute-start.22) | collective-permute-done | bytes 524320 | tf_op jit(solution)/shard_map/ppermute | solution.py:30
  122.1 5.4 %collective-permute-done.21.refs_2_ = bf16[2,64,2048]{2,1,0:T(8,128)(2,1)S(1)} collective-permute-done((bf16[2,64,2048]{2,1,0:T(8,128)(2,1)S(1)}, bf16[2,64,2048]{2,1,0:T(8,128)(2,1)S(1)}, u32[]{:S(2)}, u32[]{:S(2)}) %collective-permute-start.21) | collective-permute-done | bytes 524320 | tf_op jit(solution)/shard_map/ppermute | solution.py:30
  127.7 2.1 %input_gradient.1 = f32[32,16,512]{2,1,0:T(8,128)S(1)} custom-call(s32[3,4]{1,0:T(4,128)S(1)} %bitcast.12, s32[32]{0:T(128)S(1)} %get-tuple-element.27.places, bf16[512,2048]{1,0:T(8,128)(2,1)S(1)} %copy-done, bf16[512,2048]{1,0:T(8,128)(2,1)S(1)} %copy-done.1, bf16[2,64,2048]{2,1,0:T(8,128)(2,1)S(1)} %collective-permute-done.10.refs_0_, ...), custom_call_target="tpu_custom_call" | custom-call | flops 2147483648 | bytes 10485760 | tf_op jit(solution)/shard_map/input_gradient/pallas_call | solution.py:149
  129.9 11.0 %collective-permute-start.23 = (f32[8,32,512]{2,1,0:T(8,128)S(1)}, f32[8,32,512]{2,1,0:T(8,128)S(1)}, u32[]{:S(2)}, u32[]{:S(2)}) collective-permute-start(f32[8,32,512]{2,1,0:T(8,128)S(1)} %bitcast.15), channel_id=1, source_target_pairs={{0,1},{1,0},{2,3},{3,2},{4,5},{5,4},{6,7},{7,6},{8,9},{9,8},{10,11... | collective-permute-start | bytes 1572872 | tf_op jit(solution)/shard_map/ppermute | solution.py:298
  142.4 1.8 %collective-permute-start.27 = (bf16[1,64,2048]{2,1,0:T(8,128)(2,1)}, bf16[1,64,2048]{2,1,0:T(8,128)(2,1)S(1)}, u32[]{:S(2)}, u32[]{:S(2)}) collective-permute-start(bf16[1,64,2048]{2,1,0:T(8,128)(2,1)} %slice.157), channel_id=1, source_target_pairs={{0,192},{1,49},{16,208},{17,33},{32,224},{33,17},{48,240},{49,1},{... | collective-permute-start | bytes 786440 | tf_op jit(solution)/shard_map/ppermute | solution.py:30
  148.2 4.0 %all-to-all-start.1 = ((bf16[8,32,512]{2,1,0:T(8,128)(2,1)}), bf16[8,32,512]{2,1,0:T(8,128)(2,1)}, u32[]{:S(2)}, u32[]{:S(2)}) async-start(bf16[8,32,512]{2,1,0:T(8,128)(2,1)} %fusion.3), calls=%async_computation.1 | async-start | bytes 524288 | tf_op jit(solution)/shard_map/all_to_all | solution.py:299
  158.3 5.9 %weight_gradients.1 = (bf16[512,2048]{1,0:T(8,128)(2,1)}, bf16[512,2048]{1,0:T(8,128)(2,1)}, bf16[2048,512]{1,0:T(8,128)(2,1)}) custom-call(s32[3,4]{1,0:T(4,128)S(1)} %bitcast.13, bf16[512,1024]{1,0:T(8,128)(2,1)S(1)} %convolution_convert_fusion.tok.cot, bf16[512,1024]{1,0:T(8,128)(2,1)S(1)} %convolution_convert_fusion.tok.cot, ...), custom_call_target="tpu_custom_call" | custom-call | flops 3221225472 | bytes 12582912 | tf_op jit(solution)/shard_map/weight_gradients/pallas_call | solution.py:194
  (115 shorter events, 25.9 us)
Async XLA Ops:
  1.5 31.3 %copy-start.1 = (bf16[512,2048]{1,0:T(8,128)(2,1)S(1)}, bf16[512,2048]{1,0:T(8,128)(2,1)}, u32[]{:S(2)}) copy-start(bf16[512,2048]{1,0:T(8,128)(2,1)} %up.5) | copy-start | bytes 6291460
  26.7 4.2 %collective-permute-start = (bf16[256,1024]{1,0:T(8,128)(2,1)}, bf16[256,1024]{1,0:T(8,128)(2,1)}, u32[]{:S(2)}, u32[]{:S(2)}) collective-permute-start(bf16[256,1024]{1,0:T(8,128)(2,1)} %bitcast), channel_id=1, source_target_pairs={{0,1},{1,0},{2,3},{3,2},{4,5},{5,4},{6,7},{7,6},{8,9},{9,8},{10,11... | collective-permute-start | bytes 1572872 | tf_op jit(solution)/shard_map/ppermute | solution.py:277
  37.2 13.0 %collective-permute-start.13 = (bf16[3,64,2048]{2,1,0:T(8,128)(2,1)S(1)}, bf16[3,64,2048]{2,1,0:T(8,128)(2,1)S(1)}, u32[]{:S(2)}, u32[]{:S(2)}) collective-permute-start(bf16[3,64,2048]{2,1,0:T(8,128)(2,1)S(1)} %get-tuple-element.22), channel_id=1, source_target_pairs={{0,192},{1,49},{16,208},{17,33},{32,224},{33,17},{48,240},{49,1},{... | collective-permute-start | bytes 2359304 | tf_op jit(solution)/shard_map/ppermute | solution.py:30
  40.6 18.1 %collective-permute-start.12 = (bf16[3,64,2048]{2,1,0:T(8,128)(2,1)S(1)}, bf16[3,64,2048]{2,1,0:T(8,128)(2,1)S(1)}, u32[]{:S(2)}, u32[]{:S(2)}) collective-permute-start(bf16[3,64,2048]{2,1,0:T(8,128)(2,1)S(1)} %get-tuple-element.20), channel_id=1, source_target_pairs={{0,192},{1,49},{16,208},{17,33},{32,224},{33,17},{48,240},{49,1},{... | collective-permute-start | bytes 2359304 | tf_op jit(solution)/shard_map/ppermute | solution.py:30
  40.7 11.1 %collective-permute-start.2 = (bf16[3,64,2048]{2,1,0:T(8,128)(2,1)S(1)}, bf16[3,64,2048]{2,1,0:T(8,128)(2,1)S(1)}, u32[]{:S(2)}, u32[]{:S(2)}) collective-permute-start(bf16[3,64,2048]{2,1,0:T(8,128)(2,1)S(1)} %get-tuple-element.18), channel_id=1, source_target_pairs={{0,64},{1,17},{16,80},{17,1},{32,96},{33,49},{48,112},{49,33},{64,... | collective-permute-start | bytes 2359304 | tf_op jit(solution)/shard_map/ppermute | solution.py:30
  40.7 26.1 %collective-permute-start.1 = (bf16[3,64,2048]{2,1,0:T(8,128)(2,1)S(1)}, bf16[3,64,2048]{2,1,0:T(8,128)(2,1)S(1)}, u32[]{:S(2)}, u32[]{:S(2)}) collective-permute-start(bf16[3,64,2048]{2,1,0:T(8,128)(2,1)S(1)} %get-tuple-element.16), channel_id=1, source_target_pairs={{0,64},{1,17},{16,80},{17,1},{32,96},{33,49},{48,112},{49,33},{64,... | collective-permute-start | bytes 2359304 | tf_op jit(solution)/shard_map/ppermute | solution.py:30
  50.5 14.0 %collective-permute-start.15 = (bf16[3,32,2048]{2,1,0:T(8,128)(2,1)S(1)}, bf16[3,32,2048]{2,1,0:T(8,128)(2,1)S(1)}, u32[]{:S(2)}, u32[]{:S(2)}) collective-permute-start(bf16[3,32,2048]{2,1,0:T(8,128)(2,1)S(1)} %get-tuple-element.31), channel_id=1, source_target_pairs={{0,64},{1,17},{16,80},{17,1},{32,96},{33,49},{48,112},{49,33},{64,... | collective-permute-start | bytes 1179656 | tf_op jit(solution)/shard_map/ppermute | solution.py:30
  52.1 14.7 %collective-permute-start.4 = (bf16[3,32,2048]{2,1,0:T(8,128)(2,1)S(1)}, bf16[3,32,2048]{2,1,0:T(8,128)(2,1)S(1)}, u32[]{:S(2)}, u32[]{:S(2)}) collective-permute-start(bf16[3,32,2048]{2,1,0:T(8,128)(2,1)S(1)} %get-tuple-element.33), channel_id=1, source_target_pairs={{0,192},{1,49},{16,208},{17,33},{32,224},{33,17},{48,240},{49,1},{... | collective-permute-start | bytes 1179656 | tf_op jit(solution)/shard_map/ppermute | solution.py:30
  64.6 14.8 %collective-permute-start.16 = (f32[3,32,2048]{2,1,0:T(8,128)S(1)}, f32[3,32,2048]{2,1,0:T(8,128)S(1)}, u32[]{:S(2)}, u32[]{:S(2)}) collective-permute-start(f32[3,32,2048]{2,1,0:T(8,128)S(1)} %convert_add_fusion), channel_id=1, source_target_pairs={{0,48},{1,193},{16,32},{17,209},{32,16},{33,225},{48,0},{49,241},{... | collective-permute-start | bytes 2359304 | tf_op jit(solution)/shard_map/ppermute | solution.py:30
  66.8 7.9 %collective-permute-start.14 = (bf16[3,32,2048]{2,1,0:T(8,128)(2,1)S(1)}, bf16[3,32,2048]{2,1,0:T(8,128)(2,1)S(1)}, u32[]{:S(2)}, u32[]{:S(2)}) collective-permute-start(bf16[3,32,2048]{2,1,0:T(8,128)(2,1)S(1)} %get-tuple-element.30), channel_id=1, source_target_pairs={{0,64},{1,17},{16,80},{17,1},{32,96},{33,49},{48,112},{49,33},{64,... | collective-permute-start | bytes 1179656 | tf_op jit(solution)/shard_map/ppermute | solution.py:30
  66.9 15.4 %collective-permute-start.5 = (f32[3,32,2048]{2,1,0:T(8,128)S(1)}, f32[3,32,2048]{2,1,0:T(8,128)S(1)}, u32[]{:S(2)}, u32[]{:S(2)}) collective-permute-start(f32[3,32,2048]{2,1,0:T(8,128)S(1)} %convert_add_fusion.1), channel_id=1, source_target_pairs={{0,16},{1,65},{16,0},{17,81},{32,48},{33,97},{48,32},{49,113},{64,... | collective-permute-start | bytes 2359304 | tf_op jit(solution)/shard_map/ppermute | solution.py:30
  67.6 12.3 %collective-permute-start.3 = (bf16[3,32,2048]{2,1,0:T(8,128)(2,1)S(1)}, bf16[3,32,2048]{2,1,0:T(8,128)(2,1)S(1)}, u32[]{:S(2)}, u32[]{:S(2)}) collective-permute-start(bf16[3,32,2048]{2,1,0:T(8,128)(2,1)S(1)} %get-tuple-element.32), channel_id=1, source_target_pairs={{0,192},{1,49},{16,208},{17,33},{32,224},{33,17},{48,240},{49,1},{... | collective-permute-start | bytes 1179656 | tf_op jit(solution)/shard_map/ppermute | solution.py:30
  79.6 6.7 %collective-permute-start.17 = (f32[3,16,2048]{2,1,0:T(8,128)S(1)}, f32[3,16,2048]{2,1,0:T(8,128)S(1)}, u32[]{:S(2)}, u32[]{:S(2)}) collective-permute-start(f32[3,16,2048]{2,1,0:T(8,128)S(1)} %slice.146), channel_id=1, source_target_pairs={{0,16},{1,65},{16,0},{17,81},{32,48},{33,97},{48,32},{49,113},{64,... | collective-permute-start | bytes 1179656 | tf_op jit(solution)/shard_map/ppermute | solution.py:30
  82.5 8.2 %collective-permute-start.6 = (f32[3,16,2048]{2,1,0:T(8,128)S(1)}, f32[3,16,2048]{2,1,0:T(8,128)S(1)}, u32[]{:S(2)}, u32[]{:S(2)}) collective-permute-start(f32[3,16,2048]{2,1,0:T(8,128)S(1)} %slice.135), channel_id=1, source_target_pairs={{0,48},{1,193},{16,32},{17,209},{32,16},{33,225},{48,0},{49,241},{... | collective-permute-start | bytes 1179656 | tf_op jit(solution)/shard_map/ppermute | solution.py:30
  86.5 5.1 %collective-permute-start.18 = (bf16[3,16,2048]{2,1,0:T(8,128)(2,1)S(1)}, bf16[3,16,2048]{2,1,0:T(8,128)(2,1)S(1)}, u32[]{:S(2)}, u32[]{:S(2)}) collective-permute-start(bf16[3,16,2048]{2,1,0:T(8,128)(2,1)S(1)} %pad_maximum_fusion.1), channel_id=1, source_target_pairs={{0,16},{1,65},{16,0},{17,81},{32,48},{33,97},{48,32},{49,113},{64,... | collective-permute-start | bytes 589832 | tf_op jit(solution)/shard_map/ppermute | solution.py:30
  90.9 5.8 %collective-permute-start.7 = (bf16[3,16,2048]{2,1,0:T(8,128)(2,1)S(1)}, bf16[3,16,2048]{2,1,0:T(8,128)(2,1)S(1)}, u32[]{:S(2)}, u32[]{:S(2)}) collective-permute-start(bf16[3,16,2048]{2,1,0:T(8,128)(2,1)S(1)} %pad_maximum_fusion), channel_id=1, source_target_pairs={{0,48},{1,193},{16,32},{17,209},{32,16},{33,225},{48,0},{49,241},{... | collective-permute-start | bytes 589832 | tf_op jit(solution)/shard_map/ppermute | solution.py:30
  91.6 9.4 %collective-permute-start.19 = (bf16[3,32,2048]{2,1,0:T(8,128)(2,1)S(1)}, bf16[3,32,2048]{2,1,0:T(8,128)(2,1)S(1)}, u32[]{:S(2)}, u32[]{:S(2)}) collective-permute-start(bf16[3,32,2048]{2,1,0:T(8,128)(2,1)S(1)} %maximum_maximum_fusion.3), channel_id=1, source_target_pairs={{0,48},{1,193},{16,32},{17,209},{32,16},{33,225},{48,0},{49,241},{... | collective-permute-start | bytes 1179656 | tf_op jit(solution)/shard_map/ppermute | solution.py:30
  96.8 7.0 %collective-permute-start.8 = (bf16[3,32,2048]{2,1,0:T(8,128)(2,1)S(1)}, bf16[3,32,2048]{2,1,0:T(8,128)(2,1)S(1)}, u32[]{:S(2)}, u32[]{:S(2)}) collective-permute-start(bf16[3,32,2048]{2,1,0:T(8,128)(2,1)S(1)} %maximum_maximum_fusion.2), channel_id=1, source_target_pairs={{0,16},{1,65},{16,0},{17,81},{32,48},{33,97},{48,32},{49,113},{64,... | collective-permute-start | bytes 1179656 | tf_op jit(solution)/shard_map/ppermute | solution.py:30
  101.0 39.9 %copy-start.4 = (bf16[3,64,2048]{2,1,0:T(8,128)(2,1)}, bf16[3,64,2048]{2,1,0:T(8,128)(2,1)S(1)}, u32[]{:S(2)}) copy-start(bf16[3,64,2048]{2,1,0:T(8,128)(2,1)S(1)} %maximum_maximum_fusion.1.refs_7_.refs_11_) | copy-start | bytes 2359300
  101.0 15.4 %collective-permute-start.20 = (bf16[3,64,2048]{2,1,0:T(8,128)(2,1)S(1)}, bf16[3,64,2048]{2,1,0:T(8,128)(2,1)S(1)}, u32[]{:S(2)}, u32[]{:S(2)}) collective-permute-start(bf16[3,64,2048]{2,1,0:T(8,128)(2,1)S(1)} %maximum_maximum_fusion.1.refs_7_.refs_11_), channel_id=1, source_target_pairs={{0,64},{1,17},{16,80},{17,1},{32,96},{33,49},{48,112},{49,33},{64,... | collective-permute-start | bytes 2359304 | tf_op jit(solution)/shard_map/ppermute | solution.py:30
  103.9 37.8 %copy-start.6 = (bf16[3,64,2048]{2,1,0:T(8,128)(2,1)}, bf16[3,64,2048]{2,1,0:T(8,128)(2,1)S(1)}, u32[]{:S(2)}) copy-start(bf16[3,64,2048]{2,1,0:T(8,128)(2,1)S(1)} %maximum_maximum_fusion.refs_5_.refs_9_) | copy-start | bytes 2359300
  103.9 15.4 %collective-permute-start.9 = (bf16[3,64,2048]{2,1,0:T(8,128)(2,1)S(1)}, bf16[3,64,2048]{2,1,0:T(8,128)(2,1)S(1)}, u32[]{:S(2)}, u32[]{:S(2)}) collective-permute-start(bf16[3,64,2048]{2,1,0:T(8,128)(2,1)S(1)} %maximum_maximum_fusion.refs_5_.refs_9_), channel_id=1, source_target_pairs={{0,192},{1,49},{16,208},{17,33},{32,224},{33,17},{48,240},{49,1},{... | collective-permute-start | bytes 2359304 | tf_op jit(solution)/shard_map/ppermute | solution.py:30
  105.9 16.0 %collective-permute-start.22 = (bf16[2,64,2048]{2,1,0:T(8,128)(2,1)S(1)}, bf16[2,64,2048]{2,1,0:T(8,128)(2,1)S(1)}, u32[]{:S(2)}, u32[]{:S(2)}) collective-permute-start(bf16[2,64,2048]{2,1,0:T(8,128)(2,1)S(1)} %slice.151), channel_id=1, source_target_pairs={{0,192},{1,49},{16,208},{17,33},{32,224},{33,17},{48,240},{49,1},{... | collective-permute-start | bytes 1572872 | tf_op jit(solution)/shard_map/ppermute | solution.py:30
  106.8 15.3 %collective-permute-start.11 = (bf16[2,64,2048]{2,1,0:T(8,128)(2,1)S(1)}, bf16[2,64,2048]{2,1,0:T(8,128)(2,1)S(1)}, u32[]{:S(2)}, u32[]{:S(2)}) collective-permute-start(bf16[2,64,2048]{2,1,0:T(8,128)(2,1)S(1)} %slice.140), channel_id=1, source_target_pairs={{0,64},{1,17},{16,80},{17,1},{32,96},{33,49},{48,112},{49,33},{64,... | collective-permute-start | bytes 1572872 | tf_op jit(solution)/shard_map/ppermute | solution.py:30
  116.5 11.0 %collective-permute-start.21 = (bf16[2,64,2048]{2,1,0:T(8,128)(2,1)S(1)}, bf16[2,64,2048]{2,1,0:T(8,128)(2,1)S(1)}, u32[]{:S(2)}, u32[]{:S(2)}) collective-permute-start(bf16[2,64,2048]{2,1,0:T(8,128)(2,1)S(1)} %slice.150), channel_id=1, source_target_pairs={{0,192},{1,49},{16,208},{17,33},{32,224},{33,17},{48,240},{49,1},{... | collective-permute-start | bytes 1572872 | tf_op jit(solution)/shard_map/ppermute | solution.py:30
  119.3 8.4 %collective-permute-start.10 = (bf16[2,64,2048]{2,1,0:T(8,128)(2,1)S(1)}, bf16[2,64,2048]{2,1,0:T(8,128)(2,1)S(1)}, u32[]{:S(2)}, u32[]{:S(2)}) collective-permute-start(bf16[2,64,2048]{2,1,0:T(8,128)(2,1)S(1)} %slice.139), channel_id=1, source_target_pairs={{0,64},{1,17},{16,80},{17,1},{32,96},{33,49},{48,112},{49,33},{64,... | collective-permute-start | bytes 1572872 | tf_op jit(solution)/shard_map/ppermute | solution.py:30
  129.9 17.5 %collective-permute-start.23 = (f32[8,32,512]{2,1,0:T(8,128)S(1)}, f32[8,32,512]{2,1,0:T(8,128)S(1)}, u32[]{:S(2)}, u32[]{:S(2)}) collective-permute-start(f32[8,32,512]{2,1,0:T(8,128)S(1)} %bitcast.15), channel_id=1, source_target_pairs={{0,1},{1,0},{2,3},{3,2},{4,5},{5,4},{6,7},{7,6},{8,9},{9,8},{10,11... | collective-permute-start | bytes 1572872 | tf_op jit(solution)/shard_map/ppermute | solution.py:298
  142.4 9.8 %collective-permute-start.27 = (bf16[1,64,2048]{2,1,0:T(8,128)(2,1)}, bf16[1,64,2048]{2,1,0:T(8,128)(2,1)S(1)}, u32[]{:S(2)}, u32[]{:S(2)}) collective-permute-start(bf16[1,64,2048]{2,1,0:T(8,128)(2,1)} %slice.157), channel_id=1, source_target_pairs={{0,192},{1,49},{16,208},{17,33},{32,224},{33,17},{48,240},{49,1},{... | collective-permute-start | bytes 786440 | tf_op jit(solution)/shard_map/ppermute | solution.py:30
  144.2 8.0 %collective-permute-start.25 = (bf16[1,64,2048]{2,1,0:T(8,128)(2,1)}, bf16[1,64,2048]{2,1,0:T(8,128)(2,1)}, u32[]{:S(2)}, u32[]{:S(2)}) collective-permute-start(bf16[1,64,2048]{2,1,0:T(8,128)(2,1)} %slice.155), channel_id=1, source_target_pairs={{0,64},{1,17},{16,80},{17,1},{32,96},{33,49},{48,112},{49,33},{64,... | collective-permute-start | bytes 786440 | tf_op jit(solution)/shard_map/ppermute | solution.py:30
  145.0 7.3 %collective-permute-start.26 = (bf16[1,64,2048]{2,1,0:T(8,128)(2,1)}, bf16[1,64,2048]{2,1,0:T(8,128)(2,1)}, u32[]{:S(2)}, u32[]{:S(2)}) collective-permute-start(bf16[1,64,2048]{2,1,0:T(8,128)(2,1)} %slice.156), channel_id=1, source_target_pairs={{0,192},{1,49},{16,208},{17,33},{32,224},{33,17},{48,240},{49,1},{... | collective-permute-start | bytes 786440 | tf_op jit(solution)/shard_map/ppermute | solution.py:30
  146.6 6.3 %collective-permute-start.24 = (bf16[1,64,2048]{2,1,0:T(8,128)(2,1)}, bf16[1,64,2048]{2,1,0:T(8,128)(2,1)}, u32[]{:S(2)}, u32[]{:S(2)}) collective-permute-start(bf16[1,64,2048]{2,1,0:T(8,128)(2,1)} %slice.154), channel_id=1, source_target_pairs={{0,64},{1,17},{16,80},{17,1},{32,96},{33,49},{48,112},{49,33},{64,... | collective-permute-start | bytes 786440 | tf_op jit(solution)/shard_map/ppermute | solution.py:30
  148.2 16.0 %all-to-all-start.1 = ((bf16[8,32,512]{2,1,0:T(8,128)(2,1)}), bf16[8,32,512]{2,1,0:T(8,128)(2,1)}, u32[]{:S(2)}, u32[]{:S(2)}) async-start(bf16[8,32,512]{2,1,0:T(8,128)(2,1)} %fusion.3), calls=%async_computation.1 | async-start | bytes 524288 | tf_op jit(solution)/shard_map/all_to_all | solution.py:299
  (20 other events, 209.5 us)
